TPU v7x, 512 devices: a whole 4x8x8 slice. The times are simulated.
512 devices in a mesh: gx: 16 (over z, y_hi), gy: 32 (over x, y_lo, core).
Axes of the slice: x: 4, y: 8 (y_hi: 2, y_lo: 4; y = y_hi * 4 + y_lo), z: 8, core: 2. Of those that a mesh axis runs over, the one named last changes fastest.
Arguments:
- start_coeffs: float32 [9, 2048, 8192], P(None, 'gy', 'gx'), may hold values from -6 to 6
- section_coeffs: float32 [9, 2048, 8192], P(None, 'gy', 'gx'), may hold values from -6 to 6
- vel_x: float32 [2048, 8192], P('gy', 'gx'), may hold values from -1 to 1
- vel_y: float32 [2048, 8192], P('gy', 'gx'), may hold values from -1 to 1
Outputs:
- updated: float32 [9, 2048, 8192], P(None, 'gy', 'gx')
- filtered: float32 [9, 2048, 8192], P(None, 'gy', 'gx')
All inputs are finite; a program needn't handle non-finite values.
Results may differ from a plain program's by a relative error of at most 0.0001.
Values sent between devices are 32-bit elements; how exact they have to be, the bound alone decides.
No kernel may reach another device: no remote copies, remote signals or barrier semaphores. Data moves between devices by JAX's collectives and lax.ppermute only.
A program may use at most 64 MiB of HBM per device.

v0:
```python
import functools

import jax
import jax.numpy as jnp
import numpy as np
from jax import lax
from jax.experimental import pallas as pl
from jax.experimental.pallas import tpu as pltpu
from jax.sharding import PartitionSpec as P


HALF = np.arange(3) + 0.5
PARITY = np.array([1.0, -1.0, 1.0])
GAUSS_NODES = (
    -0.932469514203152,
    -0.6612093864662645,
    -0.2386191860831969,
    0.2386191860831969,
    0.6612093864662645,
    0.932469514203152,
)
GAUSS_WEIGHTS = (
    0.1713244923791704,
    0.3607615730481386,
    0.467913934572691,
    0.467913934572691,
    0.3607615730481386,
    0.1713244923791704,
)
HIGHEST = lax.Precision.HIGHEST
F32 = jnp.float32


def legendre_rows(points):
    return np.stack([points * 0.0 + 1.0, points, 1.5 * points * points - 0.5])


def bspline(points):
    magnitude = np.abs(points)
    return np.where(
        magnitude <= 0.5,
        0.75 - magnitude * magnitude,
        np.where(magnitude <= 1.5, 0.5 * (1.5 - magnitude) ** 2, 0.0),
    )


def kernel_value(points):
    return 1.25 * bspline(points) - 0.125 * (bspline(points + 1.0) + bspline(points - 1.0))


def siac_table():
    nodes = np.array(GAUSS_NODES)
    weights = np.array(GAUSS_WEIGHTS)
    kernel_table = np.zeros((5, 3, 3))
    for slot_index in range(5):
        offset = slot_index - 2
        for low_end, high_end in ((-1.0, 0.0), (0.0, 1.0)):
            for node_value, node_weight in zip(GAUSS_NODES, GAUSS_WEIGHTS):
                xi_value = 0.5 * (low_end + high_end) + 0.5 * (high_end - low_end) * node_value
                outer_weight = 0.5 * (high_end - low_end) * node_weight
                breaks = [-1.0, 1.0]
                for spline_knot in (-2.5, -1.5, -0.5, 0.5, 1.5, 2.5):
                    crossing = xi_value - 2.0 * offset - 2.0 * spline_knot
                    if -1.0 < crossing < 1.0:
                        breaks.append(crossing)
                breaks = sorted(breaks)
                for piece_lo, piece_hi in zip(breaks[:-1], breaks[1:]):
                    eta_points = 0.5 * (piece_lo + piece_hi) + 0.5 * (piece_hi - piece_lo) * nodes
                    eta_weights = 0.5 * (piece_hi - piece_lo) * weights
                    samples = (
                        kernel_value(0.5 * xi_value - 0.5 * eta_points - offset) * eta_weights * 0.5
                    )
                    kernel_table[slot_index] += outer_weight * np.outer(
                        legendre_rows(np.array(xi_value)), legendre_rows(eta_points) @ samples
                    )
    table = kernel_table * (np.arange(3)[None, :, None] + 0.5)
    return table.astype(np.float32).astype(np.float64)


TABLE = siac_table()


def tap(k):
    return TABLE[k + 2] if abs(k) <= 2 else np.zeros((3, 3))


def column_matrices():
    out = np.zeros((2, 128, 256))
    for group in range(4):
        base = 32 * group
        for b in range(3):
            for a in range(3):
                m_out = 3 * a + b
                for i in range(3):
                    col = base + 3 * m_out + i
                    for side, (first, near, far) in enumerate(((-2, -1, 0), (3, 2, 3))):
                        for c in range(3):
                            for j in range(2):
                                out[side, base + 2 * (3 * c + b) + j, col] += tap(first + j - i)[a, c]
                        flux = tap(near - i)[a] @ -HALF + tap(far - i)[a] @ (HALF * PARITY)
                        out[side, base + 18 + b, col] += flux
                out[0, base + 18 + b, 128 + base + m_out] += HALF[a] * PARITY[a]
                out[1, base + 18 + b, 128 + base + m_out] += -HALF[a]
    return out.astype(np.float32)


def row_matrices():
    out = np.zeros((2, 144, 64))
    for a in range(3):
        for b in range(3):
            m_out = 3 * a + b
            for i in range(3):
                for side, (first, near, far, row) in enumerate(((-2, -1, 0, i), (3, 2, 3, 5 + i))):
                    for d in range(3):
                        for j in range(2):
                            out[side, 8 * m_out + row, 9 * j + 3 * a + d] += tap(first + j - i)[b, d]
                    weight = tap(near - i)[b] @ -HALF + tap(far - i)[b] @ (HALF * PARITY)
                    for k in range(-2, 3):
                        for c in range(3):
                            out[side, 8 * m_out + row, 24 + 8 * (k + 2) + 2 + c] += tap(k)[a, c] * weight
            out[0, 72 + 8 * m_out, 24 + 16 + 2 + a] = HALF[b] * PARITY[b]
            out[1, 72 + 8 * m_out + 7, 24 + 16 + 2 + a] = -HALF[b]
    return out.astype(np.float32)


def upwind(speed, inner, outer):
    return jnp.maximum(speed, 0.0) * inner + jnp.minimum(speed, 0.0) * outer


def tile_iota(shape, dim):
    return lax.broadcasted_iota(jnp.int32, shape, dim)


def rows_of(r, count=8, first=0):
    return pl.ds(pl.multiple_of(count * r + first, 8), count)


def turned(value, shift, axis):
    shift %= value.shape[axis]
    return pltpu.roll(value, shift, axis) if shift else value


def update_terms(u, begin, speed_x, speed_y, faces_x, jumps_y):
    sixth_x, sixth_y = 0.6 * speed_x, 0.6 * speed_y
    for b in range(3):
        jump, total = faces_x(b)
        for a in range(3):
            m = 3 * a + b
            value = begin(m) * (1.0 / 3.0) + u[m] * (2.0 / 3.0)
            if a == 0:
                value = value - 0.5 * jump
            elif a == 1:
                value = value + (sixth_x * u[b] - 1.5 * total)
            else:
                value = value + (speed_x * u[3 + b] - 2.5 * jump)
            if b == 0:
                value = value - 0.5 * jumps_y(a, 0)
            elif b == 1:
                value = value + (sixth_y * u[3 * a] - 1.5 * jumps_y(a, 1))
            else:
                value = value + (speed_y * u[3 * a + 1] - 2.5 * jumps_y(a, 0))
            yield m, value


def pack_kernel(width, height, start, sect, vel_x, vel_y, west, east, send_odd, send_even, s, u, vx, vy, jumps, packed, sems):
    copies = []
    for side in range(2):
        cols = pl.ds(side * (width - 128), 128)
        copies.append([
            pltpu.make_async_copy(source.at[..., cols], target.at[side], sems.at[4 * side + n])
            for n, (source, target) in enumerate(((sect, u), (vel_y, vy), (vel_x, vx), (start, s)))
        ])
        for copy in copies[side]:
            copy.start()
    row = tile_iota((height, 128), 0)
    span = 16
    lane = tile_iota((span, 128), 1)
    for side in range(2):
        extra = 2 * side
        copies[side][0].wait()
        copies[side][1].wait()
        speeds = vy[side]
        speed = jnp.where(row == 0, 0.0, 0.1 * (speeds + pltpu.roll(speeds, 1, 0)))
        high, low = jnp.maximum(speed, 0.0), jnp.minimum(speed, 0.0)
        for a in range(3):
            even, odd = u[side, 3 * a] + u[side, 3 * a + 2], u[side, 3 * a + 1]
            north, south = even + odd, even - odd
            face = high * pltpu.roll(north, 1, 0) + low * south
            above = pltpu.roll(face, height - 1, 0)
            jumps[a] = above - face
            jumps[3 + a] = above + face
            jumps[6 + a] = jnp.where(row < height // 2, south, north)
        copies[side][2].wait()
        copies[side][3].wait()

        def cells(r, carry, side=side, extra=extra):
            rows = rows_of(r, span)
            modes = [u[side, m, rows, :] for m in range(9)]
            speed_x, speed_y = vx[side, rows, :], vy[side, rows, :]
            speed = jnp.where(lane == 0, 0.0, 0.1 * (speed_x + pltpu.roll(speed_x, 1, 1)))
            high, low = jnp.maximum(speed, 0.0), jnp.minimum(speed, 0.0)
            acc = turned(speed_x, 21 + extra // 2, 1)
            acc = jnp.where(lane == 22, turned(speed_x, 22 + extra // 2, 1), acc)
            acc = jnp.where(lane == 23, turned(speed_x, 23 + extra // 2, 1), acc)

            def put(acc, value, at, count):
                if count == 2:
                    return jnp.where((lane == at) | (lane == at + 1), turned(value, at + extra, 1), acc)
                return jnp.where(lane == at, turned(value, at + extra // 2, 1), acc)

            def faces_x(b):
                nonlocal acc
                even, odd = modes[b] + modes[6 + b], modes[3 + b]
                face = high * pltpu.roll(even + odd, 1, 1) + low * (even - odd)
                beyond = pltpu.roll(face, 127, 1)
                acc = put(acc, even + odd if side else even - odd, 18 + b, 1)
                return beyond - face, beyond + face

            terms = update_terms(
                modes,
                lambda m: s[side, m, rows, :],
                speed_x,
                speed_y,
                faces_x,
                lambda a, kind: jumps[3 * kind + a, rows, :],
            )
            for m, value in terms:
                acc = put(acc, value, 2 * m, 2)
            for a in range(3):
                acc = put(acc, jumps[6 + a, rows, :], 24 + 2 * a, 2)
            acc = put(acc, speed_y, 30, 2)
            packed[side, rows, :] = acc
            return carry

        lax.fori_loop(0, height // span, cells, 0)
    odd_column = lax.rem(lax.axis_index("gx"), 2) == 1
    slot = tile_iota((16, 128), 1)
    both = []
    for side in range(2):
        acc = packed[side, 0:16, :]
        for group in range(1, 4):
            moved = pltpu.roll(packed[side, 16 * group : 16 * group + 16, :], 32 * group, 1)
            acc = jnp.where(slot >= 32 * group, moved, acc)
        both.append(acc)
    west[...] = both[0]
    east[...] = both[1]
    send_odd[...] = jnp.where(odd_column, both[1], both[0])
    send_even[...] = jnp.where(odd_column, both[0], both[1])


def interior_kernel(width, height, start, sect, vel_x, vel_y, part, swept, traces, s, u, vx, vy, south, sems):
    chunk = 16
    tiles = height // 8
    shape = (8, width)
    lane = tile_iota(shape, 1)
    sub = tile_iota(shape, 0)
    pad = jnp.zeros((8, 128), F32)
    nothing = jnp.zeros(shape, F32)

    small = [
        pltpu.make_async_copy(vel_y, vy, sems.at[0]),
        pltpu.make_async_copy(vel_x, vx, sems.at[1]),
    ]
    small[0].start()
    copies = []
    for n in range(height // chunk):
        rows = pl.ds(chunk * n, chunk)
        copies.append(pltpu.make_async_copy(sect.at[:, rows, :], u.at[:, rows, :], sems.at[2 + n]))
        copies[n].start()
    small[1].start()
    begin = []
    for n in range(height // chunk):
        rows = pl.ds(chunk * n, chunk)
        begin.append(pltpu.make_async_copy(start.at[:, rows, :], s.at[:, rows, :], sems.at[2 + height // chunk + n]))
        begin[n].start()

    def south_faces(r, carry):
        rows = rows_of(r)
        speeds = vy[rows, :]
        turned_speed = pltpu.roll(speeds, 1, 0)
        speed = 0.1 * (speeds + jnp.where(sub == 0, carry[3], turned_speed))
        speed = jnp.where((sub == 0) & (r == 0), 0.0, speed)
        high, low = jnp.maximum(speed, 0.0), jnp.minimum(speed, 0.0)
        ahead = []
        for a in range(3):
            even, odd = u[3 * a, rows, :] + u[3 * a + 2, rows, :], u[3 * a + 1, rows, :]
            north = pltpu.roll(even + odd, 1, 0)
            south[a, rows, :] = high * jnp.where(sub == 0, carry[a], north) + low * (even - odd)
            ahead.append(north)
        return (*ahead, turned_speed)

    def shifted(field, k):
        if k == 0:
            return field[:, :width]
        return pltpu.roll(field, (-k) % (width + 128), 1)[:, :width]

    def cells(r, carry):
        rows = rows_of(r)
        after = rows_of(r, first=8)
        modes = [u[m, rows, :] for m in range(9)]
        speed_x, speed_y = vx[rows, :], vy[rows, :]
        speed = jnp.where(lane == 0, 0.0, 0.1 * (speed_x + pltpu.roll(speed_x, 1, 1)))
        high, low = jnp.maximum(speed, 0.0), jnp.minimum(speed, 0.0)
        jump_y, sum_y = [], []
        for a in range(3):
            face = south[a, rows, :]
            above = jnp.where(sub == 7, pltpu.roll(south[a, after, :], 7, 0), pltpu.roll(face, 7, 0))
            jump_y.append(above - face)
            sum_y.append(above + face)

        def faces_x(b):
            even, odd = modes[b] + modes[6 + b], modes[3 + b]
            face = high * pltpu.roll(even + odd, 1, 1) + low * (even - odd)
            beyond = pltpu.roll(face, width - 1, 1)
            return beyond - face, beyond + face

        fields = []
        terms = update_terms(
            modes, lambda m: s[m, rows, :], speed_x, speed_y, faces_x, lambda a, kind: (sum_y if kind else jump_y)[a]
        )
        for m, value in terms:
            part[m, rows, :] = value
            fields.append(jnp.concatenate([value, pad], axis=1))
            if len(fields) == 3:
                for a, out in enumerate(sweep(fields, shifted)):
                    swept[3 * a + m % 3, after, :] = out
                fields = []
        return carry

    small[0].wait()
    carry = (nothing,) * 4
    for n in range(height // chunk):
        copies[n].wait()
        carry = lax.fori_loop(n * chunk // 8, (n + 1) * chunk // 8, south_faces, carry)
    for a in range(3):
        south[a, height : height + 8, :] = nothing
        even = u[3 * a, 0:8, :] + u[3 * a + 2, 0:8, :]
        traces[a : a + 1, :] = (even - u[3 * a + 1, 0:8, :])[0:1]
        even = u[3 * a, height - 8 :, :] + u[3 * a + 2, height - 8 :, :]
        traces[4 + a : 5 + a, :] = (even + u[3 * a + 1, height - 8 :, :])[7:8]
    traces[3:4, :] = vy[0:1, :]
    traces[7:8, :] = vy[height - 1 :, :]
    for m in range(9):
        swept[m, 0:8, :] = nothing
        swept[m, height + 8 : height + 16, :] = nothing
    small[1].wait()
    for copy in begin:
        copy.wait()
    lax.fori_loop(0, tiles, cells, 0)


def sweep(fields, shifted):
    outs = [None, None, None]

    def add(i, term):
        outs[i] = term if outs[i] is None else outs[i] + term

    for c in range(3):
        for a in range(3):
            if TABLE[2, a, c] != 0.0 and (a + c) % 2 == 0:
                add(a, float(TABLE[2, a, c]) * shifted(fields[c], 0))
        for k in (1, 2):
            ahead, behind = shifted(fields[c], k), shifted(fields[c], -k)
            even, odd = ahead + behind, ahead - behind
            for a in range(3):
                add(a, float(TABLE[2 + k, a, c]) * (even if (a + c) % 2 == 0 else odd))
    return outs


def edge_kernel(width, got_odd, got_even, west, east, low_rows, high_rows, traces, matrices, send_even, send_odd, fixes, buffer):
    odd_column = lax.rem(lax.axis_index("gx"), 2) == 1
    from_west = jnp.where(odd_column, got_even[...], got_odd[...])
    from_east = jnp.where(odd_column, got_odd[...], got_even[...])
    lane16 = tile_iota((16, 128), 1)
    place = jnp.bitwise_and(lane16, 31)
    is_face = (place >= 18) & (place < 21)

    def speed_of(one, two):
        return 0.1 * (pltpu.roll(one, 125, 1) + pltpu.roll(two, 125, 1))

    own_w, own_e = west[...], east[...]
    face_w = upwind(speed_of(from_west, own_w), from_west, own_w)
    face_e = upwind(speed_of(from_east, own_e), own_e, from_east)
    fix_w = jnp.dot(jnp.where(is_face, face_w, from_west), matrices[0], precision=HIGHEST, preferred_element_type=F32)
    fix_e = jnp.dot(jnp.where(is_face, face_e, from_east), matrices[1], precision=HIGHEST, preferred_element_type=F32)
    fixes[0] = fix_w[:, :128]
    fixes[1] = fix_e[:, :128]
    fixes[2] = fix_w[:, 128:]
    fixes[3] = fix_e[:, 128:]

    lane = tile_iota((8, 128), 1)
    buffer[...] = jnp.zeros_like(buffer)
    for side, tile in enumerate((low_rows, high_rows)):
        half, turn = (0, 0) if side == 0 else (1, 32)
        first = 0 if side == 0 else 6
        near_w = fix_w[8 * half : 8 * half + 8, :128]
        near_e = fix_e[8 * half : 8 * half + 8, :128]
        for m in range(9):
            turn_w, turn_e = (turn - 3 * m) % 128, (turn + 125 - 3 * m) % 128
            add_w = jnp.where(lane < 3, pltpu.roll(near_w, turn_w, 1) if turn_w else near_w, 0.0)
            add_e = jnp.where(lane >= 125, pltpu.roll(near_e, turn_e, 1) if turn_e else near_e, 0.0)
            left = tile[m, :, :128] + add_w
            right = tile[m, :, width - 128 :] + add_e
            middle = tile[m, :, 128 : width - 128]
            for j in range(2):
                row = slice(9 * j + m, 9 * j + m + 1)
                at = slice(first + j, first + j + 1)
                buffer[side, row, 0:128] = left[at]
                buffer[side, row, 128 : width - 128] = middle[at]
                buffer[side, row, width - 128 : width] = right[at]
        for a in range(4):
            row = slice(18 + a, 19 + a)
            buffer[side, row, 0:width] = traces[4 * side + a : 4 * side + a + 1, :]
            source = slice(0, 8) if side == 0 else slice(8, 16)
            base = 24 + 2 * a + (0 if side == 0 else 96)
            line = slice(0, 1) if side == 0 else slice(7, 8)
            left = pltpu.roll(from_west[source], (126 - base) % 128, 1)
            right = pltpu.roll(from_east[source], (-base) % 128, 1)
            halo = jnp.where(lane >= 126, left, jnp.where(lane < 2, right, 0.0))
            buffer[side, row, width : width + 128] = halo[line]
    odd_row = lax.rem(lax.axis_index("gy"), 2) == 1
    for j in range(3):
        rows = slice(8 * j, 8 * j + 8)
        low, high = buffer[0, rows, :], buffer[1, rows, :]
        send_even[rows, :] = jnp.where(odd_row, low, high)
        send_odd[rows, :] = jnp.where(odd_row, high, low)


def finish_kernel(width, height, part, swept, fixes, updated, filtered, edges, new, out, tall, sems):
    lane = tile_iota((8, 128), 1)
    tiles = height // 8
    last = slice(width - 128, width)

    for r in range(tiles):
        group, half = r // 2, r % 2
        tile = [fixes[n, 8 * half : 8 * half + 8, :] for n in range(4)]
        rows = slice(8 * r, 8 * r + 8)
        for m in range(9):
            left = jnp.where(lane == 0, turned(tile[2], -32 * group - m, 1), 0.0)
            right = jnp.where(lane == 127, turned(tile[3], 127 - 32 * group - m, 1), 0.0)
            target = edges.at[0 if r == 0 else 1, m] if r in (0, tiles - 1) else new.at[m, rows]
            target[:, 0:128] = part[m, rows, 0:128] + left
            target[:, 128 : width - 128] = part[m, rows, 128 : width - 128]
            target[:, last] = part[m, rows, last] + right
    inner = slice(8, height - 8)
    first_copy = pltpu.make_async_copy(new.at[:, inner], updated.at[:, inner], sems.at[0])
    first_copy.start()

    for r in range(tiles):
        group, half = r // 2, r % 2
        near_w, near_e = (fixes[n, 8 * half : 8 * half + 8, :] for n in range(2))
        rows = slice(8 * r + 8, 8 * r + 16)
        for m in range(9):
            left = jnp.where(lane < 3, turned(near_w, -32 * group - 3 * m, 1), 0.0)
            right = jnp.where(lane >= 125, turned(near_e, 125 - 32 * group - 3 * m, 1), 0.0)
            tall[0, m, rows, :] = swept[m, rows, 0:128] + left
            tall[1, m, rows, :] = swept[m, rows, last] + right
    pad = jnp.zeros((8, 128), F32)
    for side in range(2):
        for m in range(9):
            tall[side, m, 0:8, :] = pad
            tall[side, m, height + 8 : height + 16, :] = pad

    def filtered_copy(a):
        modes = pl.ds(3 * a, 3)
        return pltpu.make_async_copy(out.at[modes, inner], filtered.at[modes, inner], sems.at[1 + a])

    def body(a, carry):
        for r in range(tiles):
            rows = slice(8 * r, 8 * r + 8)
            for cols, source in (
                (slice(0, 128), lambda d, at: tall[0, 3 * a + d, at, :]),
                (slice(128, width - 128), lambda d, at: swept[3 * a + d, at, 128 : width - 128]),
                (last, lambda d, at: tall[1, 3 * a + d, at, :]),
            ):
                def shifted(d, k):
                    return source(d, slice(8 * r + 8 + k, 8 * r + 16 + k))

                for b, value in enumerate(sweep([0, 1, 2], shifted)):
                    if r in (0, tiles - 1):
                        edges[0 if r == 0 else 1, 9 + 3 * a + b, :, cols] = value
                    else:
                        out[3 * a + b, rows, cols] = value
        filtered_copy(a).start()
        return carry

    lax.fori_loop(0, 3, body, 0)
    first_copy.wait()
    for a in range(3):
        filtered_copy(a).wait()


def row_fix_kernel(width, height, got_even, got_odd, sent_even, sent_odd, matrices, edges, updated_in, filtered_in, updated, filtered, tiles, sems):
    odd_row = lax.rem(lax.axis_index("gy"), 2)
    copies = []
    for side in range(2):
        use_odd = lax.rem(side + odd_row, 2) == 0
        got = jnp.where(use_odd, got_odd[...], got_even[...])
        own = jnp.where(use_odd, sent_odd[16:24, :], sent_even[16:24, :])
        edge = got[16:24]
        speed = 0.1 * (edge[5:6] + own[5:6])
        inner, outer = (edge, own) if side == 0 else (own, edge)
        face = jnp.maximum(speed, 0.0) * inner + jnp.minimum(speed, 0.0) * outer
        pieces = [got[:, :width]]
        for k in range(-2, 3):
            pieces.append(turned(face, -k, 1)[:, :width])
        fix = jnp.dot(matrices[side], jnp.concatenate(pieces, axis=0), precision=HIGHEST, preferred_element_type=F32)
        for m in range(9):
            tiles[side, 0, m] = edges[side, m] + fix[72 + 8 * m : 80 + 8 * m]
            tiles[side, 1, m] = edges[side, 9 + m] + fix[8 * m : 8 * m + 8]
        rows = slice(0, 8) if side == 0 else slice(height - 8, height)
        for n, target in enumerate((updated, filtered)):
            copies.append(pltpu.make_async_copy(tiles.at[side, n], target.at[:, rows], sems.at[2 * side + n]))
            copies[-1].start()
    for copy in copies:
        copy.wait()


def swap_pairs(count, offset):
    pairs = []
    for i in range(offset, count + offset, 2):
        one, two = i % count, (i + 1) % count
        pairs += [(one, two), (two, one)]
    return pairs


VMEM = pl.BlockSpec(memory_space=pltpu.VMEM)
HBM = pl.BlockSpec(memory_space=pltpu.HBM)
DMA = pltpu.SemaphoreType.DMA


def call(kernel, out_shape, work, grant=24 << 20, **options):
    return pl.pallas_call(
        kernel,
        out_shape=out_shape,
        compiler_params=pltpu.CompilerParams(vmem_limit_bytes=grant),
        cost_estimate=pl.CostEstimate(flops=work[0], bytes_accessed=work[1], transcendentals=0),
        **options,
    )


def per_device(start_coeffs, section_coeffs, vel_x, vel_y):
    height, width = vel_x.shape
    shape = jax.ShapeDtypeStruct
    full = shape((9, height, width), F32)
    pack = shape((16, 128), F32)
    inputs = (start_coeffs, section_coeffs, vel_x, vel_y)
    west, east, send_odd, send_even = call(
        functools.partial(pack_kernel, width, height),
        (pack,) * 4,
        (20_000_000, 1_400_000),
        grant=62 << 20,
        in_specs=[HBM] * 4,
        out_specs=(VMEM,) * 4,
        scratch_shapes=[
            pltpu.VMEM((2, 9, height, 128), F32),
            pltpu.VMEM((2, 9, height, 128), F32),
            pltpu.VMEM((2, height, 128), F32),
            pltpu.VMEM((2, height, 128), F32),
            pltpu.VMEM((9, height, 128), F32),
            pltpu.VMEM((2, height, 128), F32),
            DMA((8,)),
        ],
    )(*inputs)
    x_odd, x_even = swap_pairs(lax.axis_size("gx"), 1), swap_pairs(lax.axis_size("gx"), 0)
    y_odd, y_even = swap_pairs(lax.axis_size("gy"), 1), swap_pairs(lax.axis_size("gy"), 0)
    got_odd = lax.ppermute(send_odd, "gx", x_odd)
    got_even = lax.ppermute(send_even, "gx", x_even)
    part, swept, traces = call(
        functools.partial(interior_kernel, width, height),
        (full, shape((9, height + 16, width), F32), shape((8, width), F32)),
        (120_000_000, 5_000_000),
        in_specs=[HBM] * 4,
        out_specs=(VMEM,) * 3,
        scratch_shapes=[
            pltpu.VMEM((9, height, width), F32),
            pltpu.VMEM((9, height, width), F32),
            pltpu.VMEM((height, width), F32),
            pltpu.VMEM((height, width), F32),
            pltpu.VMEM((3, height + 8, width), F32),
            DMA((10,)),
        ],
    )(*inputs)
    tall = shape((24, width + 128), F32)
    whole = lambda *dims: pl.BlockSpec(dims, lambda i: (0,) * len(dims))
    send_y_even, send_y_odd, fixes = call(
        functools.partial(edge_kernel, width),
        (tall, tall, shape((4, 16, 128), F32)),
        (4_000_000, 1_000_000),
        grid=(1,),
        in_specs=[whole(16, 128)] * 4
        + [
            pl.BlockSpec((9, 8, width), lambda i: (0, 1, 0)),
            pl.BlockSpec((9, 8, width), lambda i: (0, height // 8, 0)),
            whole(8, width),
            whole(2, 128, 256),
        ],
        out_specs=(whole(24, width + 128), whole(24, width + 128), whole(4, 16, 128)),
        scratch_shapes=[pltpu.VMEM((2, 24, width + 128), F32)],
    )(got_odd, got_even, west, east, swept, swept, traces, jnp.asarray(column_matrices()))
    got_y_even = lax.ppermute(send_y_even, "gy", y_even)
    got_y_odd = lax.ppermute(send_y_odd, "gy", y_odd)
    updated, filtered, edges = call(
        functools.partial(finish_kernel, width, height),
        (full, full, shape((2, 18, 8, width), F32)),
        (60_000_000, 4_000_000),
        in_specs=[VMEM] * 3,
        out_specs=(HBM, HBM, VMEM),
        scratch_shapes=[
            pltpu.VMEM((9, height, width), F32),
            pltpu.VMEM((9, height, width), F32),
            pltpu.VMEM((2, 9, height + 16, 128), F32),
            DMA((4,)),
        ],
    )(part, swept, fixes)
    return call(
        functools.partial(row_fix_kernel, width, height),
        (full, full),
        (4_000_000, 1_000_000),
        in_specs=[VMEM] * 6 + [HBM] * 2,
        out_specs=(HBM, HBM),
        input_output_aliases={6: 0, 7: 1},
        scratch_shapes=[pltpu.VMEM((2, 2, 9, 8, width), F32), DMA((4,))],
    )(got_y_even, got_y_odd, send_y_even, send_y_odd, jnp.asarray(row_matrices()), edges, updated, filtered)


def solution(mesh):
    placed = (P(None, "gy", "gx"), P(None, "gy", "gx"), P("gy", "gx"), P("gy", "gx"))
    return jax.shard_map(
        per_device,
        mesh=mesh,
        in_specs=placed,
        out_specs=(P(None, "gy", "gx"), P(None, "gy", "gx")),
        check_vma=False,
    )
```

profile of v0, /device:TPU:2, one launch (start us, length us, event | category | flops | bytes accessed | tf_op | source)
XLA Modules:
  0.0 42.5 jit_solution(6445327574395450007)
XLA Ops:
  0.6 0.0 copy-start
  0.6 0.0 copy-start.2
  0.6 0.0 copy-start.3
  0.7 3.9 %shard_map.77 = (f32[16,128]{1,0:T(8,128)}, f32[16,128]{1,0:T(8,128)}, f32[16,128]{1,0:T(8,128)}, f32[16,128]{1,0:T(8,128)}) custom-call(f32[9,64,512]{2,1,0:T(8,128)} %start.3, f32[9,64,512]{2,1,0:T(8,128)} %sect.3, f32[64,512]{1,0:T(8,128)} %vel_x.3, f32[64,512]{1,0:T(8,128)} %vel_y.3), custom_call_target="tpu_custom_call" | custom-call | flops 20000000 | bytes 1400000 | tf_op jit(solution)/shard_map/pallas_call | solution.py:548
  4.6 16.2 %collective-permute-start = (f32[16,128]{1,0:T(8,128)}, f32[16,128]{1,0:T(8,128)S(1)}, u32[]{:S(2)}, u32[]{:S(2)}) collective-permute-start(f32[16,128]{1,0:T(8,128)} %get-tuple-element.15), channel_id=1, source_target_pairs={{32,64},{64,32},{96,128},{128,96},{160,192},{192,160},{224,256},{2... | collective-permute-start | bytes 24584 | tf_op jit(solution)/shard_map/ppermute | solution.py:567
  20.8 1.9 %collective-permute-start.1 = (f32[16,128]{1,0:T(8,128)}, f32[16,128]{1,0:T(8,128)S(1)}, u32[]{:S(2)}, u32[]{:S(2)}) collective-permute-start(f32[16,128]{1,0:T(8,128)} %get-tuple-element.16), channel_id=1, source_target_pairs={{0,32},{32,0},{64,96},{96,64},{128,160},{160,128},{192,224},{224,1... | collective-permute-start | bytes 24584 | tf_op jit(solution)/shard_map/ppermute | solution.py:568
  22.7 0.0 copy-done
  22.7 0.0 copy-done.2
  22.7 0.0 copy-done.3
  22.8 0.0 copy-start.1
  22.8 1.3 %copy-done.1 = f32[9,64,512]{2,1,0:T(8,128)S(1)} copy-done((f32[9,64,512]{2,1,0:T(8,128)S(1)}, f32[9,64,512]{2,1,0:T(8,128)}, u32[]{:S(2)}) %copy-start.1) | copy-done | bytes 1179672
  24.0 0.0 copy-start.4
  24.0 0.0 copy-start.6
  24.0 0.0 copy-start.7
  24.0 3.9 %shard_map.78 = (f32[9,64,512]{2,1,0:T(8,128)S(1)}, f32[9,80,512]{2,1,0:T(8,128)S(1)}, f32[8,512]{1,0:T(8,128)S(1)}) custom-call(f32[9,64,512]{2,1,0:T(8,128)S(1)} %copy-done, f32[9,64,512]{2,1,0:T(8,128)S(1)} %copy-done.1, f32[64,512]{1,0:T(8,128)S(1)} %copy-done.2, f32[64,512]{1,0:T(8,128)S(1)} %copy-done.3), custom_call_target="tpu_custom_call" | custom-call | flops 120000000 | bytes 5000000 | tf_op jit(solution)/shard_map/pallas_call | solution.py:569
  28.0 0.0 collective-permute-done.got_odd
  28.0 2.5 %collective-permute-done.1.got_even = f32[16,128]{1,0:T(8,128)S(1)} collective-permute-done((f32[16,128]{1,0:T(8,128)}, f32[16,128]{1,0:T(8,128)S(1)}, u32[]{:S(2)}, u32[]{:S(2)}) %collective-permute-start.1) | collective-permute-done | bytes 8224 | tf_op jit(solution)/shard_map/ppermute | solution.py:568
  30.5 0.0 copy-done.4
  30.5 0.0 copy-done.6
  30.5 0.0 copy-done.7
  30.5 0.4 shard_map.79
  30.9 1.9 %collective-permute-start.2 = (f32[24,640]{1,0:T(8,128)S(1)}, f32[24,640]{1,0:T(8,128)S(1)}, u32[]{:S(2)}, u32[]{:S(2)}) collective-permute-start(f32[24,640]{1,0:T(8,128)S(1)} %get-tuple-element.21.sent_even), channel_id=1, source_target_pairs={{0,1},{1,0},{2,3},{3,2},{4,5},{5,4},{6,7},{7,6},{8,9},{9,8},{10,11... | collective-permute-start | bytes 184328 | tf_op jit(solution)/shard_map/ppermute | solution.py:601
  32.8 2.9 %collective-permute-start.3 = (f32[24,640]{1,0:T(8,128)S(1)}, f32[24,640]{1,0:T(8,128)S(1)}, u32[]{:S(2)}, u32[]{:S(2)}) collective-permute-start(f32[24,640]{1,0:T(8,128)S(1)} %get-tuple-element.22.sent_odd), channel_id=1, source_target_pairs={{1,2},{2,1},{3,4},{4,3},{5,6},{6,5},{7,8},{8,7},{9,10},{10,9},{11,... | collective-permute-start | bytes 184328 | tf_op jit(solution)/shard_map/ppermute | solution.py:602
  35.7 0.0 copy-start.5
  35.7 2.4 %shard_map.80 = (f32[9,64,512]{2,1,0:T(8,128)}, f32[9,64,512]{2,1,0:T(8,128)}, f32[2,18,8,512]{3,2,1,0:T(8,128)S(1)}) custom-call(f32[9,64,512]{2,1,0:T(8,128)S(1)} %get-tuple-element.23.part, f32[9,80,512]{2,1,0:T(8,128)S(1)} %get-tuple-element.19.low_rows.high_rows.swept, f32[4,16,128]{2,1,0:T(8,128)S(1)} %get-tuple-element.24.fixes), custom_call_target="tpu_custom_call" | custom-call | flops 60000000 | bytes 4000000 | tf_op jit(solution)/shard_map/pallas_call | solution.py:603
  38.2 0.0 collective-permute-done.2.got_even
  38.2 2.9 %collective-permute-done.3.got_odd = f32[24,640]{1,0:T(8,128)S(1)} collective-permute-done((f32[24,640]{1,0:T(8,128)S(1)}, f32[24,640]{1,0:T(8,128)S(1)}, u32[]{:S(2)}, u32[]{:S(2)}) %collective-permute-start.3) | collective-permute-done | bytes 61472 | tf_op jit(solution)/shard_map/ppermute | solution.py:602
  41.1 0.0 copy-done.5
  41.1 1.4 %shard_map.81 = (f32[9,64,512]{2,1,0:T(8,128)}, f32[9,64,512]{2,1,0:T(8,128)}) custom-call(f32[24,640]{1,0:T(8,128)S(1)} %collective-permute-done.2.got_even, f32[24,640]{1,0:T(8,128)S(1)} %collective-permute-done.3.got_odd, f32[24,640]{1,0:T(8,128)S(1)} %get-tuple-element.21.sent_even, ...), custom_call_target="tpu_custom_call", output_to_operand_aliasing={{0}: (6, {}), {1}: (7, {})} | custom-call | flops 4000000 | bytes 1000000 | tf_op jit(solution)/shard_map/pallas_call | solution.py:616
Async XLA Ops:
  0.6 22.1 %copy-start = (f32[9,64,512]{2,1,0:T(8,128)S(1)}, f32[9,64,512]{2,1,0:T(8,128)}, u32[]{:S(2)}) copy-start(f32[9,64,512]{2,1,0:T(8,128)} %start.3) | copy-start | bytes 3538948
  0.6 22.1 %copy-start.2 = (f32[64,512]{1,0:T(8,128)S(1)}, f32[64,512]{1,0:T(8,128)}, u32[]{:S(2)}) copy-start(f32[64,512]{1,0:T(8,128)} %vel_x.3) | copy-start | bytes 393220
  0.6 22.1 %copy-start.3 = (f32[64,512]{1,0:T(8,128)S(1)}, f32[64,512]{1,0:T(8,128)}, u32[]{:S(2)}) copy-start(f32[64,512]{1,0:T(8,128)} %vel_y.3) | copy-start | bytes 393220
  4.6 23.4 %collective-permute-start = (f32[16,128]{1,0:T(8,128)}, f32[16,128]{1,0:T(8,128)S(1)}, u32[]{:S(2)}, u32[]{:S(2)}) collective-permute-start(f32[16,128]{1,0:T(8,128)} %get-tuple-element.15), channel_id=1, source_target_pairs={{32,64},{64,32},{96,128},{128,96},{160,192},{192,160},{224,256},{2... | collective-permute-start | bytes 24584 | tf_op jit(solution)/shard_map/ppermute | solution.py:567
  20.8 9.7 %collective-permute-start.1 = (f32[16,128]{1,0:T(8,128)}, f32[16,128]{1,0:T(8,128)S(1)}, u32[]{:S(2)}, u32[]{:S(2)}) collective-permute-start(f32[16,128]{1,0:T(8,128)} %get-tuple-element.16), channel_id=1, source_target_pairs={{0,32},{32,0},{64,96},{96,64},{128,160},{160,128},{192,224},{224,1... | collective-permute-start | bytes 24584 | tf_op jit(solution)/shard_map/ppermute | solution.py:568
  22.8 1.3 %copy-start.1 = (f32[9,64,512]{2,1,0:T(8,128)S(1)}, f32[9,64,512]{2,1,0:T(8,128)}, u32[]{:S(2)}) copy-start(f32[9,64,512]{2,1,0:T(8,128)} %sect.3) | copy-start | bytes 3538948
  24.0 6.4 %copy-start.4 = (f32[2,128,256]{2,1,0:T(8,128)S(1)}, f32[2,128,256]{2,1,0:T(8,128)}, u32[]{:S(2)}) copy-start(f32[2,128,256]{2,1,0:T(8,128)} %constant.4.clone.matrices) | copy-start | bytes 786436
  24.0 6.4 %copy-start.6 = (f32[16,128]{1,0:T(8,128)S(1)}, f32[16,128]{1,0:T(8,128)}, u32[]{:S(2)}) copy-start(f32[16,128]{1,0:T(8,128)} %get-tuple-element.17.west) | copy-start | bytes 24580
  24.0 6.4 %copy-start.7 = (f32[16,128]{1,0:T(8,128)S(1)}, f32[16,128]{1,0:T(8,128)}, u32[]{:S(2)}) copy-start(f32[16,128]{1,0:T(8,128)} %get-tuple-element.18.east) | copy-start | bytes 24580
  30.9 7.3 %collective-permute-start.2 = (f32[24,640]{1,0:T(8,128)S(1)}, f32[24,640]{1,0:T(8,128)S(1)}, u32[]{:S(2)}, u32[]{:S(2)}) collective-permute-start(f32[24,640]{1,0:T(8,128)S(1)} %get-tuple-element.21.sent_even), channel_id=1, source_target_pairs={{0,1},{1,0},{2,3},{3,2},{4,5},{5,4},{6,7},{7,6},{8,9},{9,8},{10,11... | collective-permute-start | bytes 184328 | tf_op jit(solution)/shard_map/ppermute | solution.py:601
  32.8 8.2 %collective-permute-start.3 = (f32[24,640]{1,0:T(8,128)S(1)}, f32[24,640]{1,0:T(8,128)S(1)}, u32[]{:S(2)}, u32[]{:S(2)}) collective-permute-start(f32[24,640]{1,0:T(8,128)S(1)} %get-tuple-element.22.sent_odd), channel_id=1, source_target_pairs={{1,2},{2,1},{3,4},{4,3},{5,6},{6,5},{7,8},{8,7},{9,10},{10,9},{11,... | collective-permute-start | bytes 184328 | tf_op jit(solution)/shard_map/ppermute | solution.py:602
  35.7 5.3 %copy-start.5 = (f32[2,144,64]{2,1,0:T(8,128)S(1)}, f32[2,144,64]{2,1,0:T(8,128)}, u32[]{:S(2)}) copy-start(f32[2,144,64]{2,1,0:T(8,128)} %constant.5.clone.matrices) | copy-start | bytes 221188
where the time goes:
time: 42.8 us; the launch traced here: 42.5 us
  starting transfers between devices  22.9 us (54%)
  Pallas kernels  12.1 us (28%)
  waiting for transfers between devices  5.36 us (13%)
  local copies, waits for them, and re-layouts  1.3 us (3%)
  between operations  0.78 us (2%)
    ppermute x1, starting transfers between devices, per_device(): got_odd = lax.ppermute(send_odd, 'gx', x_odd)  16.2 us
    pallas_call x1, Pallas kernels, per_device(): call(functools.partial(interior_kernel, width, height), (full, shape((9,...  3.92 us
    pallas_call x1, Pallas kernels, per_device(): call(functools.partial(pack_kernel, width, height), (pack,) * 4, (2000000...  3.91 us
    ppermute x1, starting transfers between devices, per_device(): got_y_odd = lax.ppermute(send_y_odd, 'gy', y_odd)  2.89 us
    ppermute x1, waiting for transfers between devices, per_device(): got_y_odd = lax.ppermute(send_y_odd, 'gy', y_odd)  2.87 us
    ppermute x1, waiting for transfers between devices, per_device(): got_even = lax.ppermute(send_even, 'gx', x_even)  2.49 us
    pallas_call x1, Pallas kernels, per_device(): call(functools.partial(finish_kernel, width, height), (full, full, shape(...  2.44 us
    ppermute x1, starting transfers between devices, per_device(): got_y_even = lax.ppermute(send_y_even, 'gy', y_even)  1.92 us
  transfers between devices with their start and end apart: 4, of which 2 were waited for; matrix products, arithmetic and copies ran while one was open for 0% of the time, Pallas kernels for 15%

commit v1 on v0

--- a/solution.py
+++ b/solution.py
@@ -162,93 +162,101 @@
             yield m, value
 
 
-def pack_kernel(width, height, start, sect, vel_x, vel_y, west, east, send_odd, send_even, s, u, vx, vy, jumps, packed, sems):
+def pack_kernel(width, height, start, sect, vel_x, vel_y, west, east, send_odd, send_even, raw, dense, sems):
     copies = []
     for side in range(2):
         cols = pl.ds(side * (width - 128), 128)
-        copies.append([
-            pltpu.make_async_copy(source.at[..., cols], target.at[side], sems.at[4 * side + n])
-            for n, (source, target) in enumerate(((sect, u), (vel_y, vy), (vel_x, vx), (start, s)))
-        ])
-        for copy in copies[side]:
-            copy.start()
-    row = tile_iota((height, 128), 0)
-    span = 16
-    lane = tile_iota((span, 128), 1)
-    for side in range(2):
-        extra = 2 * side
-        copies[side][0].wait()
-        copies[side][1].wait()
-        speeds = vy[side]
-        speed = jnp.where(row == 0, 0.0, 0.1 * (speeds + pltpu.roll(speeds, 1, 0)))
-        high, low = jnp.maximum(speed, 0.0), jnp.minimum(speed, 0.0)
-        for a in range(3):
-            even, odd = u[side, 3 * a] + u[side, 3 * a + 2], u[side, 3 * a + 1]
-            north, south = even + odd, even - odd
-            face = high * pltpu.roll(north, 1, 0) + low * south
-            above = pltpu.roll(face, height - 1, 0)
-            jumps[a] = above - face
-            jumps[3 + a] = above + face
-            jumps[6 + a] = jnp.where(row < height // 2, south, north)
-        copies[side][2].wait()
-        copies[side][3].wait()
-
-        def cells(r, carry, side=side, extra=extra):
-            rows = rows_of(r, span)
-            modes = [u[side, m, rows, :] for m in range(9)]
-            speed_x, speed_y = vx[side, rows, :], vy[side, rows, :]
-            speed = jnp.where(lane == 0, 0.0, 0.1 * (speed_x + pltpu.roll(speed_x, 1, 1)))
-            high, low = jnp.maximum(speed, 0.0), jnp.minimum(speed, 0.0)
-            acc = turned(speed_x, 21 + extra // 2, 1)
-            acc = jnp.where(lane == 22, turned(speed_x, 22 + extra // 2, 1), acc)
-            acc = jnp.where(lane == 23, turned(speed_x, 23 + extra // 2, 1), acc)
-
-            def put(acc, value, at, count):
-                if count == 2:
-                    return jnp.where((lane == at) | (lane == at + 1), turned(value, at + extra, 1), acc)
-                return jnp.where(lane == at, turned(value, at + extra // 2, 1), acc)
-
-            def faces_x(b):
-                nonlocal acc
-                even, odd = modes[b] + modes[6 + b], modes[3 + b]
-                face = high * pltpu.roll(even + odd, 1, 1) + low * (even - odd)
-                beyond = pltpu.roll(face, 127, 1)
-                acc = put(acc, even + odd if side else even - odd, 18 + b, 1)
-                return beyond - face, beyond + face
-
-            terms = update_terms(
-                modes,
-                lambda m: s[side, m, rows, :],
-                speed_x,
-                speed_y,
-                faces_x,
-                lambda a, kind: jumps[3 * kind + a, rows, :],
-            )
-            for m, value in terms:
-                acc = put(acc, value, 2 * m, 2)
-            for a in range(3):
-                acc = put(acc, jumps[6 + a, rows, :], 24 + 2 * a, 2)
-            acc = put(acc, speed_y, 30, 2)
-            packed[side, rows, :] = acc
-            return carry
-
-        lax.fori_loop(0, height // span, cells, 0)
+        for n, (source, at) in enumerate(((sect, pl.ds(0, 9)), (start, pl.ds(9, 9)), (vel_x, 18), (vel_y, 19))):
+            copies.append(pltpu.make_async_copy(source.at[..., cols], raw.at[side, at], sems.at[4 * side + n]))
+            copies[-1].start()
+    for copy in copies:
+        copy.wait()
+    tiles = height // 8
+    lane = tile_iota((8, 128), 1)
+    sub = tile_iota((8, 128), 0)
+    spot = jnp.bitwise_and(lane, 15)
+
+    def gather(m, carry):
+        first = acc = None
+        for r in range(tiles):
+            rows = slice(8 * r, 8 * r + 8)
+            moved = turned(jnp.where(lane < 64, raw[0, m, rows, :], raw[1, m, rows, :]), 16 * r, 1)
+            if r == 0:
+                first = acc = moved
+            else:
+                acc = jnp.where(lane >= 16 * r - 8, moved, acc)
+        acc = jnp.where(lane >= 120, first, acc)
+        dense[m] = jnp.where(spot >= 8, pltpu.roll(acc, 16, 1), acc)
+        return carry
+
+    lax.fori_loop(0, 20, gather, 0, unroll=4)
+
+    def below(value):
+        value = pltpu.roll(value, 1, 0)
+        return jnp.where(sub == 0, pltpu.roll(value, 16, 1), value)
+
+    def above(value):
+        value = pltpu.roll(value, 7, 0)
+        return jnp.where(sub == 7, pltpu.roll(value, 112, 1), value)
+
+    modes = [dense[m] for m in range(9)]
+    speed_x, speed_y = dense[18], dense[19]
+    speed = jnp.where((sub == 0) & (lane < 16), 0.0, 0.1 * (speed_y + below(speed_y)))
+    high, low = jnp.maximum(speed, 0.0), jnp.minimum(speed, 0.0)
+    jumps, side_traces = [], []
+    for a in range(3):
+        even, odd = modes[3 * a] + modes[3 * a + 2], modes[3 * a + 1]
+        north, south = even + odd, even - odd
+        face = high * below(north) + low * south
+        face_north = above(face)
+        jumps.append((face_north - face, face_north + face))
+        side_traces.append(jnp.where(lane < 64, south, north))
+    side_traces.append(speed_y)
+    speed = jnp.where(spot == 0, 0.0, 0.1 * (speed_x + pltpu.roll(speed_x, 1, 1)))
+    high, low = jnp.maximum(speed, 0.0), jnp.minimum(speed, 0.0)
+    column_traces = []
+
+    def faces_x(b):
+        even, odd = modes[b] + modes[6 + b], modes[3 + b]
+        face = high * pltpu.roll(even + odd, 1, 1) + low * (even - odd)
+        beyond = pltpu.roll(face, 127, 1)
+        column_traces.append((even - odd, even + odd))
+        return beyond - face, beyond + face
+
+    values = dict(
+        update_terms(modes, lambda m: dense[9 + m], speed_x, speed_y, faces_x, lambda a, kind: jumps[a][kind])
+    )
     odd_column = lax.rem(lax.axis_index("gx"), 2) == 1
-    slot = tile_iota((16, 128), 1)
     both = []
     for side in range(2):
-        acc = packed[side, 0:16, :]
-        for group in range(1, 4):
-            moved = pltpu.roll(packed[side, 16 * group : 16 * group + 16, :], 32 * group, 1)
-            acc = jnp.where(slot >= 32 * group, moved, acc)
-        both.append(acc)
-    west[...] = both[0]
-    east[...] = both[1]
-    send_odd[...] = jnp.where(odd_column, both[1], both[0])
-    send_even[...] = jnp.where(odd_column, both[0], both[1])
-
-
-def interior_kernel(width, height, start, sect, vel_x, vel_y, part, swept, traces, s, u, vx, vy, south, sems):
+        two, one = (0, 0) if side == 0 else (14, 15)
+        low_slots = turned(values[0], -two, 1)
+        for m in range(1, 8):
+            low_slots = jnp.where(spot >= 2 * m, turned(values[m], 2 * m - two, 1), low_slots)
+        high_slots = turned(values[8], -two, 1)
+        singles = [column_traces[b][side] for b in range(3)] + [speed_x] * 3
+        for n, value in enumerate(singles):
+            high_slots = jnp.where(spot >= 2 + n, turned(value, 2 + n - one, 1), high_slots)
+        for n, value in enumerate(side_traces):
+            high_slots = jnp.where(spot >= 8 + 2 * n, turned(value, 8 + 2 * n - two, 1), high_slots)
+        half = jnp.bitwise_and(lane, 16) == 0
+        both.append((
+            jnp.where(half, low_slots, pltpu.roll(high_slots, 16, 1)),
+            jnp.where(half, pltpu.roll(low_slots, 112, 1), high_slots),
+        ))
+    for half in range(2):
+        rows = slice(8 * half, 8 * half + 8)
+        west[rows, :] = both[0][half]
+        east[rows, :] = both[1][half]
+        send_odd[rows, :] = jnp.where(odd_column, both[1][half], both[0][half])
+        send_even[rows, :] = jnp.where(odd_column, both[0][half], both[1][half])
+
+
+def interior_kernel(
+    width, height, start, sect, vel_x, vel_y, updated, filtered, part, swept, traces, edges, s, u, vx, vy, south, new, out, sems
+):
+    middle = slice(128, width - 128)
+    inner = slice(8, height - 8)
     chunk = 16
     tiles = height // 8
     shape = (8, width)
@@ -319,7 +327,9 @@
             modes, lambda m: s[m, rows, :], speed_x, speed_y, faces_x, lambda a, kind: (sum_y if kind else jump_y)[a]
         )
         for m, value in terms:
-            part[m, rows, :] = value
+            part[0, m, rows, :] = value[:, :128]
+            new[m, rows, :] = value[:, middle]
+            part[1, m, rows, :] = value[:, width - 128 :]
             fields.append(jnp.concatenate([value, pad], axis=1))
             if len(fields) == 3:
                 for a, out in enumerate(sweep(fields, shifted)):
@@ -347,6 +357,34 @@
     for copy in begin:
         copy.wait()
     lax.fori_loop(0, tiles, cells, 0)
+    new_copy = pltpu.make_async_copy(new.at[:, inner], updated.at[:, inner, middle], sems.at[10])
+    new_copy.start()
+    for m in range(9):
+        edges[0, m] = new[m, 0:8, :]
+        edges[1, m] = new[m, height - 8 :, :]
+
+    def out_copy(a):
+        modes = pl.ds(3 * a, 3)
+        return pltpu.make_async_copy(out.at[modes, inner], filtered.at[modes, inner, middle], sems.at[11 + a])
+
+    def columns(a, carry):
+        for r in range(tiles):
+
+            def taken(d, k):
+                return swept[3 * a + d, 8 * r + 8 + k : 8 * r + 16 + k, middle]
+
+            for b, value in enumerate(sweep([0, 1, 2], taken)):
+                if r in (0, tiles - 1):
+                    edges[0 if r == 0 else 1, 9 + 3 * a + b] = value
+                else:
+                    out[3 * a + b, 8 * r : 8 * r + 8, :] = value
+        out_copy(a).start()
+        return carry
+
+    lax.fori_loop(0, 3, columns, 0)
+    new_copy.wait()
+    for a in range(3):
+        out_copy(a).wait()
 
 
 def sweep(fields, shifted):
@@ -426,71 +464,58 @@
         send_odd[rows, :] = jnp.where(odd_row, high, low)
 
 
-def finish_kernel(width, height, part, swept, fixes, updated, filtered, edges, new, out, tall, sems):
+def finish_kernel(width, height, part, swept, fixes, updated_in, filtered_in, updated, filtered, edges, new, out, tall, sems):
     lane = tile_iota((8, 128), 1)
     tiles = height // 8
-    last = slice(width - 128, width)
-
-    for r in range(tiles):
-        group, half = r // 2, r % 2
-        tile = [fixes[n, 8 * half : 8 * half + 8, :] for n in range(4)]
-        rows = slice(8 * r, 8 * r + 8)
-        for m in range(9):
-            left = jnp.where(lane == 0, turned(tile[2], -32 * group - m, 1), 0.0)
-            right = jnp.where(lane == 127, turned(tile[3], 127 - 32 * group - m, 1), 0.0)
-            target = edges.at[0 if r == 0 else 1, m] if r in (0, tiles - 1) else new.at[m, rows]
-            target[:, 0:128] = part[m, rows, 0:128] + left
-            target[:, 128 : width - 128] = part[m, rows, 128 : width - 128]
-            target[:, last] = part[m, rows, last] + right
     inner = slice(8, height - 8)
-    first_copy = pltpu.make_async_copy(new.at[:, inner], updated.at[:, inner], sems.at[0])
-    first_copy.start()
-
-    for r in range(tiles):
-        group, half = r // 2, r % 2
-        near_w, near_e = (fixes[n, 8 * half : 8 * half + 8, :] for n in range(2))
-        rows = slice(8 * r + 8, 8 * r + 16)
-        for m in range(9):
-            left = jnp.where(lane < 3, turned(near_w, -32 * group - 3 * m, 1), 0.0)
-            right = jnp.where(lane >= 125, turned(near_e, 125 - 32 * group - 3 * m, 1), 0.0)
-            tall[0, m, rows, :] = swept[m, rows, 0:128] + left
-            tall[1, m, rows, :] = swept[m, rows, last] + right
+    columns = (slice(0, 128), slice(width - 128, width))
     pad = jnp.zeros((8, 128), F32)
+    copies = []
     for side in range(2):
+        target = 127 * side
+        near = lane < 3 if side == 0 else lane >= 125
         for m in range(9):
             tall[side, m, 0:8, :] = pad
             tall[side, m, height + 8 : height + 16, :] = pad
-
-    def filtered_copy(a):
-        modes = pl.ds(3 * a, 3)
-        return pltpu.make_async_copy(out.at[modes, inner], filtered.at[modes, inner], sems.at[1 + a])
+        for r in range(tiles):
+            group, half = r // 2, r % 2
+            strip = slice(8 * half, 8 * half + 8)
+            rows = slice(8 * r, 8 * r + 8)
+            for m in range(9):
+                fix = jnp.where(lane == target, turned(fixes[2 + side, strip, :], target - 32 * group - m, 1), 0.0)
+                value = part[side, m, rows, :] + fix
+                if r in (0, tiles - 1):
+                    edges[side, 0 if r == 0 else 1, m] = value
+                else:
+                    new[side, m, rows, :] = value
+                fix = turned(fixes[side, strip, :], 125 * side - 32 * group - 3 * m, 1)
+                tall[side, m, 8 * r + 8 : 8 * r + 16, :] = swept[m, 8 * r + 8 : 8 * r + 16, columns[side]] + jnp.where(near, fix, 0.0)
+        copies.append(pltpu.make_async_copy(new.at[side, :, inner], updated.at[:, inner, columns[side]], sems.at[side]))
+        copies[-1].start()
 
     def body(a, carry):
-        for r in range(tiles):
-            rows = slice(8 * r, 8 * r + 8)
-            for cols, source in (
-                (slice(0, 128), lambda d, at: tall[0, 3 * a + d, at, :]),
-                (slice(128, width - 128), lambda d, at: swept[3 * a + d, at, 128 : width - 128]),
-                (last, lambda d, at: tall[1, 3 * a + d, at, :]),
-            ):
-                def shifted(d, k):
-                    return source(d, slice(8 * r + 8 + k, 8 * r + 16 + k))
-
-                for b, value in enumerate(sweep([0, 1, 2], shifted)):
+        for side in range(2):
+            for r in range(tiles):
+
+                def taken(d, k):
+                    return tall[side, 3 * a + d, 8 * r + 8 + k : 8 * r + 16 + k, :]
+
+                for b, value in enumerate(sweep([0, 1, 2], taken)):
                     if r in (0, tiles - 1):
-                        edges[0 if r == 0 else 1, 9 + 3 * a + b, :, cols] = value
+                        edges[side, 0 if r == 0 else 1, 9 + 3 * a + b] = value
                     else:
-                        out[3 * a + b, rows, cols] = value
-        filtered_copy(a).start()
+                        out[side, 3 * a + b, 8 * r : 8 * r + 8, :] = value
         return carry
 
     lax.fori_loop(0, 3, body, 0)
-    first_copy.wait()
-    for a in range(3):
-        filtered_copy(a).wait()
-
-
-def row_fix_kernel(width, height, got_even, got_odd, sent_even, sent_odd, matrices, edges, updated_in, filtered_in, updated, filtered, tiles, sems):
+    for side in range(2):
+        copies.append(pltpu.make_async_copy(out.at[side, :, inner], filtered.at[:, inner, columns[side]], sems.at[2 + side]))
+        copies[-1].start()
+    for copy in copies:
+        copy.wait()
+
+
+def row_fix_kernel(width, height, got_even, got_odd, sent_even, sent_odd, matrices, middle, outer, updated_in, filtered_in, updated, filtered, tiles, sems):
     odd_row = lax.rem(lax.axis_index("gy"), 2)
     copies = []
     for side in range(2):
@@ -499,15 +524,17 @@
         own = jnp.where(use_odd, sent_odd[16:24, :], sent_even[16:24, :])
         edge = got[16:24]
         speed = 0.1 * (edge[5:6] + own[5:6])
-        inner, outer = (edge, own) if side == 0 else (own, edge)
-        face = jnp.maximum(speed, 0.0) * inner + jnp.minimum(speed, 0.0) * outer
+        face = upwind(speed, edge, own) if side == 0 else upwind(speed, own, edge)
         pieces = [got[:, :width]]
         for k in range(-2, 3):
             pieces.append(turned(face, -k, 1)[:, :width])
         fix = jnp.dot(matrices[side], jnp.concatenate(pieces, axis=0), precision=HIGHEST, preferred_element_type=F32)
-        for m in range(9):
-            tiles[side, 0, m] = edges[side, m] + fix[72 + 8 * m : 80 + 8 * m]
-            tiles[side, 1, m] = edges[side, 9 + m] + fix[8 * m : 8 * m + 8]
+        for n, first in enumerate((72, 0)):
+            for m in range(9):
+                add = fix[first + 8 * m : first + 8 * m + 8]
+                tiles[side, n, m, :, 0:128] = outer[0, side, 9 * n + m] + add[:, :128]
+                tiles[side, n, m, :, 128 : width - 128] = middle[side, 9 * n + m] + add[:, 128 : width - 128]
+                tiles[side, n, m, :, width - 128 : width] = outer[1, side, 9 * n + m] + add[:, width - 128 :]
         rows = slice(0, 8) if side == 0 else slice(height - 8, height)
         for n, target in enumerate((updated, filtered)):
             copies.append(pltpu.make_async_copy(tiles.at[side, n], target.at[:, rows], sems.at[2 * side + n]))
@@ -545,40 +572,41 @@
     full = shape((9, height, width), F32)
     pack = shape((16, 128), F32)
     inputs = (start_coeffs, section_coeffs, vel_x, vel_y)
+    inputs = tuple(pltpu.with_memory_space_constraint(x, pltpu.HBM) for x in inputs)
     west, east, send_odd, send_even = call(
         functools.partial(pack_kernel, width, height),
         (pack,) * 4,
         (20_000_000, 1_400_000),
-        grant=62 << 20,
         in_specs=[HBM] * 4,
         out_specs=(VMEM,) * 4,
-        scratch_shapes=[
-            pltpu.VMEM((2, 9, height, 128), F32),
-            pltpu.VMEM((2, 9, height, 128), F32),
-            pltpu.VMEM((2, height, 128), F32),
-            pltpu.VMEM((2, height, 128), F32),
-            pltpu.VMEM((9, height, 128), F32),
-            pltpu.VMEM((2, height, 128), F32),
-            DMA((8,)),
-        ],
+        scratch_shapes=[pltpu.VMEM((2, 20, height, 128), F32), pltpu.VMEM((20, 8, 128), F32), DMA((8,))],
     )(*inputs)
     x_odd, x_even = swap_pairs(lax.axis_size("gx"), 1), swap_pairs(lax.axis_size("gx"), 0)
     y_odd, y_even = swap_pairs(lax.axis_size("gy"), 1), swap_pairs(lax.axis_size("gy"), 0)
     got_odd = lax.ppermute(send_odd, "gx", x_odd)
     got_even = lax.ppermute(send_even, "gx", x_even)
-    part, swept, traces = call(
+    updated, filtered, part, swept, traces, middle = call(
         functools.partial(interior_kernel, width, height),
-        (full, shape((9, height + 16, width), F32), shape((8, width), F32)),
+        (
+            full,
+            full,
+            shape((2, 9, height, 128), F32),
+            shape((9, height + 16, width), F32),
+            shape((8, width), F32),
+            shape((2, 18, 8, width - 256), F32),
+        ),
         (120_000_000, 5_000_000),
         in_specs=[HBM] * 4,
-        out_specs=(VMEM,) * 3,
+        out_specs=(HBM, HBM) + (VMEM,) * 4,
         scratch_shapes=[
             pltpu.VMEM((9, height, width), F32),
             pltpu.VMEM((9, height, width), F32),
             pltpu.VMEM((height, width), F32),
             pltpu.VMEM((height, width), F32),
             pltpu.VMEM((3, height + 8, width), F32),
-            DMA((10,)),
+            pltpu.VMEM((9, height, width - 256), F32),
+            pltpu.VMEM((9, height, width - 256), F32),
+            DMA((14,)),
         ],
     )(*inputs)
     tall = shape((24, width + 128), F32)
@@ -600,28 +628,29 @@
     )(got_odd, got_even, west, east, swept, swept, traces, jnp.asarray(column_matrices()))
     got_y_even = lax.ppermute(send_y_even, "gy", y_even)
     got_y_odd = lax.ppermute(send_y_odd, "gy", y_odd)
-    updated, filtered, edges = call(
+    updated, filtered, outer = call(
         functools.partial(finish_kernel, width, height),
-        (full, full, shape((2, 18, 8, width), F32)),
+        (full, full, shape((2, 2, 18, 8, 128), F32)),
         (60_000_000, 4_000_000),
-        in_specs=[VMEM] * 3,
+        in_specs=[VMEM] * 3 + [HBM] * 2,
         out_specs=(HBM, HBM, VMEM),
+        input_output_aliases={3: 0, 4: 1},
         scratch_shapes=[
-            pltpu.VMEM((9, height, width), F32),
-            pltpu.VMEM((9, height, width), F32),
+            pltpu.VMEM((2, 9, height, 128), F32),
+            pltpu.VMEM((2, 9, height, 128), F32),
             pltpu.VMEM((2, 9, height + 16, 128), F32),
             DMA((4,)),
         ],
-    )(part, swept, fixes)
+    )(part, swept, fixes, updated, filtered)
     return call(
         functools.partial(row_fix_kernel, width, height),
         (full, full),
         (4_000_000, 1_000_000),
-        in_specs=[VMEM] * 6 + [HBM] * 2,
+        in_specs=[VMEM] * 7 + [HBM] * 2,
         out_specs=(HBM, HBM),
-        input_output_aliases={6: 0, 7: 1},
+        input_output_aliases={7: 0, 8: 1},
         scratch_shapes=[pltpu.VMEM((2, 2, 9, 8, width), F32), DMA((4,))],
-    )(got_y_even, got_y_odd, send_y_even, send_y_odd, jnp.asarray(row_matrices()), edges, updated, filtered)
+    )(got_y_even, got_y_odd, send_y_even, send_y_odd, jnp.asarray(row_matrices()), middle, outer, updated, filtered)
 
 
 def solution(mesh):

time: 42.8 us -> 42.4 us (level)
  the two profiles are of different devices: /device:TPU:2 before, /device:TPU:63 now
where the time goes in v1:
time: 42.4 us; the launch traced here: 42.1 us
  starting transfers between devices  25.3 us (60%)
  Pallas kernels  12.6 us (30%)
  waiting for transfers between devices  3.45 us (8%)
  between operations  0.74 us (2%)
    ppermute x1, starting transfers between devices, per_device(): got_even = lax.ppermute(send_even, 'gx', x_even)  11.6 us
    pallas_call x1, Pallas kernels, per_device(): call(functools.partial(interior_kernel, width, height), (full, full, shap...  6.66 us
    ppermute x1, starting transfers between devices, per_device(): got_odd = lax.ppermute(send_odd, 'gx', x_odd)  6.24 us
    ppermute x1, starting transfers between devices, per_device(): got_y_odd = lax.ppermute(send_y_odd, 'gy', y_odd)  4.36 us
    ppermute x1, waiting for transfers between devices, per_device(): got_y_odd = lax.ppermute(send_y_odd, 'gy', y_odd)  3.44 us
    ppermute x1, starting transfers between devices, per_device(): got_y_even = lax.ppermute(send_y_even, 'gy', y_even)  3.14 us
    pallas_call x1, Pallas kernels, per_device(): call(functools.partial(pack_kernel, width, height), (pack,) * 4, (2000000...  2.51 us
    pallas_call x1, Pallas kernels, per_device(): call(functools.partial(finish_kernel, width, height), (full, full, shape(...  1.61 us
  transfers between devices with their start and end apart: 4, of which 1 were waited for; matrix products, arithmetic and copies ran while one was open for 0% of the time, Pallas kernels for 20%

profile of v1, /device:TPU:63, one launch (start us, length us, event | category | flops | bytes accessed | tf_op | source)
XLA Modules:
  0.0 42.1 jit_solution(15610825580861232891)
XLA Ops:
  0.6 2.5 %shard_map.77 = (f32[16,128]{1,0:T(8,128)S(1)}, f32[16,128]{1,0:T(8,128)S(1)}, f32[16,128]{1,0:T(8,128)S(1)}, f32[16,128]{1,0:T(8,128)S(1)}) custom-call(f32[9,64,512]{2,1,0:T(8,128)} %start.3, f32[9,64,512]{2,1,0:T(8,128)} %sect.3, f32[64,512]{1,0:T(8,128)} %vel_x.3, f32[64,512]{1,0:T(8,128)} %vel_y.3), custom_call_target="tpu_custom_call" | custom-call | flops 20000000 | bytes 1400000 | tf_op jit(solution)/shard_map/pallas_call | solution.py:576
  3.1 6.2 %collective-permute-start = (f32[16,128]{1,0:T(8,128)S(1)}, f32[16,128]{1,0:T(8,128)S(1)}, u32[]{:S(2)}, u32[]{:S(2)}) collective-permute-start(f32[16,128]{1,0:T(8,128)S(1)} %get-tuple-element.18), channel_id=1, source_target_pairs={{32,64},{64,32},{96,128},{128,96},{160,192},{192,160},{224,256},{2... | collective-permute-start | bytes 24584 | tf_op jit(solution)/shard_map/ppermute | solution.py:586
  9.4 0.0 copy-start
  9.4 11.6 %collective-permute-start.1 = (f32[16,128]{1,0:T(8,128)S(1)}, f32[16,128]{1,0:T(8,128)S(1)}, u32[]{:S(2)}, u32[]{:S(2)}) collective-permute-start(f32[16,128]{1,0:T(8,128)S(1)} %get-tuple-element.19), channel_id=1, source_target_pairs={{0,32},{32,0},{64,96},{96,64},{128,160},{160,128},{192,224},{224,1... | collective-permute-start | bytes 24584 | tf_op jit(solution)/shard_map/ppermute | solution.py:587
  21.0 6.7 %shard_map.78 = (f32[9,64,512]{2,1,0:T(8,128)}, f32[9,64,512]{2,1,0:T(8,128)}, f32[2,9,64,128]{3,2,1,0:T(8,128)S(1)}, f32[9,80,512]{2,1,0:T(8,128)S(1)}, f32[8,5...) custom-call(f32[9,64,512]{2,1,0:T(8,128)} %start.3, f32[9,64,512]{2,1,0:T(8,128)} %sect.3, f32[64,512]{1,0:T(8,128)} %vel_x.3, ...), custom_call_target="tpu_custom_call" | custom-call | flops 120000000 | bytes 5000000 | tf_op jit(solution)/shard_map/pallas_call | solution.py:588
  27.6 0.0 collective-permute-done.got_odd
  27.6 0.0 collective-permute-done.1.got_even
  27.7 0.0 copy-done
  27.7 0.4 shard_map.79
  28.1 3.1 %collective-permute-start.2 = (f32[24,640]{1,0:T(8,128)S(1)}, f32[24,640]{1,0:T(8,128)S(1)}, u32[]{:S(2)}, u32[]{:S(2)}) collective-permute-start(f32[24,640]{1,0:T(8,128)S(1)} %get-tuple-element.24.sent_even), channel_id=1, source_target_pairs={{0,1},{1,0},{2,3},{3,2},{4,5},{5,4},{6,7},{7,6},{8,9},{9,8},{10,11... | collective-permute-start | bytes 184328 | tf_op jit(solution)/shard_map/ppermute | solution.py:629
  31.2 4.4 %collective-permute-start.3 = (f32[24,640]{1,0:T(8,128)S(1)}, f32[24,640]{1,0:T(8,128)S(1)}, u32[]{:S(2)}, u32[]{:S(2)}) collective-permute-start(f32[24,640]{1,0:T(8,128)S(1)} %get-tuple-element.25.sent_odd), channel_id=1, source_target_pairs={{1,2},{2,1},{3,4},{4,3},{5,6},{6,5},{7,8},{8,7},{9,10},{10,9},{11,... | collective-permute-start | bytes 184328 | tf_op jit(solution)/shard_map/ppermute | solution.py:630
  35.6 0.0 copy-start.1
  35.6 1.6 %shard_map.80 = (f32[9,64,512]{2,1,0:T(8,128)}, f32[9,64,512]{2,1,0:T(8,128)}, f32[2,2,18,8,128]{4,3,2,1,0:T(8,128)S(1)}) custom-call(f32[2,9,64,128]{3,2,1,0:T(8,128)S(1)} %get-tuple-element.27.part, f32[9,80,512]{2,1,0:T(8,128)S(1)} %get-tuple-element.22.low_rows.high_rows.swept, ...), custom_call_target="tpu_custom_call", output_to_operand_aliasing={{0}: (3, {}), {1}: (4, {})} | custom-call | flops 60000000 | bytes 4000000 | tf_op jit(solution)/shard_map/pallas_call | solution.py:631
  37.2 0.0 collective-permute-done.2.got_even
  37.2 3.4 %collective-permute-done.3.got_odd = f32[24,640]{1,0:T(8,128)S(1)} collective-permute-done((f32[24,640]{1,0:T(8,128)S(1)}, f32[24,640]{1,0:T(8,128)S(1)}, u32[]{:S(2)}, u32[]{:S(2)}) %collective-permute-start.3) | collective-permute-done | bytes 61472 | tf_op jit(solution)/shard_map/ppermute | solution.py:630
  40.7 0.0 copy-done.1
  40.7 1.4 %shard_map.81 = (f32[9,64,512]{2,1,0:T(8,128)}, f32[9,64,512]{2,1,0:T(8,128)}) custom-call(f32[24,640]{1,0:T(8,128)S(1)} %collective-permute-done.2.got_even, f32[24,640]{1,0:T(8,128)S(1)} %collective-permute-done.3.got_odd, f32[24,640]{1,0:T(8,128)S(1)} %get-tuple-element.24.sent_even, ...), custom_call_target="tpu_custom_call", output_to_operand_aliasing={{0}: (7, {}), {1}: (8, {})} | custom-call | flops 4000000 | bytes 1000000 | tf_op jit(solution)/shard_map/pallas_call | solution.py:645
Async XLA Ops:
  3.1 24.5 %collective-permute-start = (f32[16,128]{1,0:T(8,128)S(1)}, f32[16,128]{1,0:T(8,128)S(1)}, u32[]{:S(2)}, u32[]{:S(2)}) collective-permute-start(f32[16,128]{1,0:T(8,128)S(1)} %get-tuple-element.18), channel_id=1, source_target_pairs={{32,64},{64,32},{96,128},{128,96},{160,192},{192,160},{224,256},{2... | collective-permute-start | bytes 24584 | tf_op jit(solution)/shard_map/ppermute | solution.py:586
  9.4 18.3 %copy-start = (f32[2,128,256]{2,1,0:T(8,128)S(1)}, f32[2,128,256]{2,1,0:T(8,128)}, u32[]{:S(2)}) copy-start(f32[2,128,256]{2,1,0:T(8,128)} %constant.4.clone.matrices) | copy-start | bytes 786436
  9.4 18.2 %collective-permute-start.1 = (f32[16,128]{1,0:T(8,128)S(1)}, f32[16,128]{1,0:T(8,128)S(1)}, u32[]{:S(2)}, u32[]{:S(2)}) collective-permute-start(f32[16,128]{1,0:T(8,128)S(1)} %get-tuple-element.19), channel_id=1, source_target_pairs={{0,32},{32,0},{64,96},{96,64},{128,160},{160,128},{192,224},{224,1... | collective-permute-start | bytes 24584 | tf_op jit(solution)/shard_map/ppermute | solution.py:587
  28.1 9.1 %collective-permute-start.2 = (f32[24,640]{1,0:T(8,128)S(1)}, f32[24,640]{1,0:T(8,128)S(1)}, u32[]{:S(2)}, u32[]{:S(2)}) collective-permute-start(f32[24,640]{1,0:T(8,128)S(1)} %get-tuple-element.24.sent_even), channel_id=1, source_target_pairs={{0,1},{1,0},{2,3},{3,2},{4,5},{5,4},{6,7},{7,6},{8,9},{9,8},{10,11... | collective-permute-start | bytes 184328 | tf_op jit(solution)/shard_map/ppermute | solution.py:629
  31.2 9.4 %collective-permute-start.3 = (f32[24,640]{1,0:T(8,128)S(1)}, f32[24,640]{1,0:T(8,128)S(1)}, u32[]{:S(2)}, u32[]{:S(2)}) collective-permute-start(f32[24,640]{1,0:T(8,128)S(1)} %get-tuple-element.25.sent_odd), channel_id=1, source_target_pairs={{1,2},{2,1},{3,4},{4,3},{5,6},{6,5},{7,8},{8,7},{9,10},{10,9},{11,... | collective-permute-start | bytes 184328 | tf_op jit(solution)/shard_map/ppermute | solution.py:630
  35.6 5.1 %copy-start.1 = (f32[2,144,64]{2,1,0:T(8,128)S(1)}, f32[2,144,64]{2,1,0:T(8,128)}, u32[]{:S(2)}) copy-start(f32[2,144,64]{2,1,0:T(8,128)} %constant.5.clone.matrices) | copy-start | bytes 221188

commit v2 on v1

--- a/solution.py
+++ b/solution.py
@@ -164,13 +164,11 @@
 
 def pack_kernel(width, height, start, sect, vel_x, vel_y, west, east, send_odd, send_even, raw, dense, sems):
     copies = []
-    for side in range(2):
-        cols = pl.ds(side * (width - 128), 128)
-        for n, (source, at) in enumerate(((sect, pl.ds(0, 9)), (start, pl.ds(9, 9)), (vel_x, 18), (vel_y, 19))):
-            copies.append(pltpu.make_async_copy(source.at[..., cols], raw.at[side, at], sems.at[4 * side + n]))
+    for n, (source, at) in enumerate(((sect, pl.ds(0, 9)), (vel_x, 9), (vel_y, 10), (start, pl.ds(11, 9)))):
+        for side in range(2):
+            cols = pl.ds(side * (width - 128), 128)
+            copies.append(pltpu.make_async_copy(source.at[..., cols], raw.at[side, at], sems.at[2 * n + side]))
             copies[-1].start()
-    for copy in copies:
-        copy.wait()
     tiles = height // 8
     lane = tile_iota((8, 128), 1)
     sub = tile_iota((8, 128), 0)
@@ -189,7 +187,12 @@
         dense[m] = jnp.where(spot >= 8, pltpu.roll(acc, 16, 1), acc)
         return carry
 
-    lax.fori_loop(0, 20, gather, 0, unroll=4)
+    for copy in copies[:2]:
+        copy.wait()
+    lax.fori_loop(0, 9, gather, 0, unroll=3)
+    for copy in copies[2:]:
+        copy.wait()
+    lax.fori_loop(9, 20, gather, 0, unroll=4)
 
     def below(value):
         value = pltpu.roll(value, 1, 0)
@@ -200,7 +203,7 @@
         return jnp.where(sub == 7, pltpu.roll(value, 112, 1), value)
 
     modes = [dense[m] for m in range(9)]
-    speed_x, speed_y = dense[18], dense[19]
+    speed_x, speed_y = dense[9], dense[10]
     speed = jnp.where((sub == 0) & (lane < 16), 0.0, 0.1 * (speed_y + below(speed_y)))
     high, low = jnp.maximum(speed, 0.0), jnp.minimum(speed, 0.0)
     jumps, side_traces = [], []
@@ -224,7 +227,7 @@
         return beyond - face, beyond + face
 
     values = dict(
-        update_terms(modes, lambda m: dense[9 + m], speed_x, speed_y, faces_x, lambda a, kind: jumps[a][kind])
+        update_terms(modes, lambda m: dense[11 + m], speed_x, speed_y, faces_x, lambda a, kind: jumps[a][kind])
     )
     odd_column = lax.rem(lax.axis_index("gx"), 2) == 1
     both = []
@@ -252,7 +255,39 @@
         send_even[rows, :] = jnp.where(odd_column, both[0][half], both[1][half])
 
 
-def interior_kernel(
+def sweep_rows(tiles, load, store):
+    sub = tile_iota((8, 128), 0)
+    cache = {}
+
+    def rolled(d, r, amount):
+        if not 0 <= r < tiles:
+            return 0.0
+        if (d, r, amount) not in cache:
+            cache[d, r, amount] = turned(load(d, r), amount, 0)
+        return cache[d, r, amount]
+
+    for r in range(tiles):
+
+        def taken(d, k):
+            if k == 0:
+                return rolled(d, r, 0)
+            if k > 0:
+                return jnp.where(sub < 8 - k, rolled(d, r, 8 - k), rolled(d, r + 1, 8 - k))
+            return jnp.where(sub >= -k, rolled(d, r, -k), rolled(d, r - 1, -k))
+
+        for b, value in enumerate(sweep([0, 1, 2], taken)):
+            store(b, r, value)
+
+
+def interior_kernel(width, height, early, *refs):
+    inputs, rest = refs[:4], refs[4 if early else 10 :]
+
+    @pl.when((lax.axis_index("gx") == 0) == early)
+    def _():
+        interior(width, height, *inputs, *rest)
+
+
+def interior(
     width, height, start, sect, vel_x, vel_y, updated, filtered, part, swept, traces, edges, s, u, vx, vy, south, new, out, sems
 ):
     middle = slice(128, width - 128)
@@ -262,7 +297,6 @@
     shape = (8, width)
     lane = tile_iota(shape, 1)
     sub = tile_iota(shape, 0)
-    pad = jnp.zeros((8, 128), F32)
     nothing = jnp.zeros(shape, F32)
 
     small = [
@@ -297,10 +331,30 @@
             ahead.append(north)
         return (*ahead, turned_speed)
 
-    def shifted(field, k):
-        if k == 0:
-            return field[:, :width]
-        return pltpu.roll(field, (-k) % (width + 128), 1)[:, :width]
+    pieces = width // 128
+    narrow = tile_iota((8, 128), 1)
+
+    def sweep_columns(fields, store):
+        cache = {}
+
+        def rolled(c, j, amount):
+            if not 0 <= j < pieces:
+                return 0.0
+            if (c, j, amount) not in cache:
+                cache[c, j, amount] = turned(fields[c][:, 128 * j : 128 * j + 128], amount, 1)
+            return cache[c, j, amount]
+
+        for j in range(pieces):
+
+            def taken(c, k):
+                if k == 0:
+                    return rolled(c, j, 0)
+                if k > 0:
+                    return jnp.where(narrow < 128 - k, rolled(c, j, 128 - k), rolled(c, j + 1, 128 - k))
+                return jnp.where(narrow >= -k, rolled(c, j, -k), rolled(c, j - 1, -k))
+
+            for a, value in enumerate(sweep([0, 1, 2], taken)):
+                store(a, slice(128 * j, 128 * j + 128), value)
 
     def cells(r, carry):
         rows = rows_of(r)
@@ -330,10 +384,13 @@
             part[0, m, rows, :] = value[:, :128]
             new[m, rows, :] = value[:, middle]
             part[1, m, rows, :] = value[:, width - 128 :]
-            fields.append(jnp.concatenate([value, pad], axis=1))
+            fields.append(value)
             if len(fields) == 3:
-                for a, out in enumerate(sweep(fields, shifted)):
-                    swept[3 * a + m % 3, after, :] = out
+
+                def keep(a, cols, value, b=m % 3):
+                    swept[3 * a + b, rows, cols] = value
+
+                sweep_columns(fields, keep)
                 fields = []
         return carry
 
@@ -350,13 +407,10 @@
         traces[4 + a : 5 + a, :] = (even + u[3 * a + 1, height - 8 :, :])[7:8]
     traces[3:4, :] = vy[0:1, :]
     traces[7:8, :] = vy[height - 1 :, :]
-    for m in range(9):
-        swept[m, 0:8, :] = nothing
-        swept[m, height + 8 : height + 16, :] = nothing
     small[1].wait()
-    for copy in begin:
-        copy.wait()
-    lax.fori_loop(0, tiles, cells, 0)
+    for n in range(height // chunk):
+        begin[n].wait()
+        lax.fori_loop(n * chunk // 8, (n + 1) * chunk // 8, cells, 0)
     new_copy = pltpu.make_async_copy(new.at[:, inner], updated.at[:, inner, middle], sems.at[10])
     new_copy.start()
     for m in range(9):
@@ -368,16 +422,20 @@
         return pltpu.make_async_copy(out.at[modes, inner], filtered.at[modes, inner, middle], sems.at[11 + a])
 
     def columns(a, carry):
-        for r in range(tiles):
-
-            def taken(d, k):
-                return swept[3 * a + d, 8 * r + 8 + k : 8 * r + 16 + k, middle]
-
-            for b, value in enumerate(sweep([0, 1, 2], taken)):
+        def column(j, carry):
+            source = pl.ds(pl.multiple_of(128 * j + 128, 128), 128)
+            target = pl.ds(pl.multiple_of(128 * j, 128), 128)
+
+            def store(b, r, value):
                 if r in (0, tiles - 1):
-                    edges[0 if r == 0 else 1, 9 + 3 * a + b] = value
+                    edges[0 if r == 0 else 1, 9 + 3 * a + b, :, target] = value
                 else:
-                    out[3 * a + b, 8 * r : 8 * r + 8, :] = value
+                    out[3 * a + b, 8 * r : 8 * r + 8, target] = value
+
+            sweep_rows(tiles, lambda d, r: swept[3 * a + d, 8 * r : 8 * r + 8, source], store)
+            return carry
+
+        lax.fori_loop(0, pieces - 2, column, 0)
         out_copy(a).start()
         return carry
 
@@ -469,14 +527,10 @@
     tiles = height // 8
     inner = slice(8, height - 8)
     columns = (slice(0, 128), slice(width - 128, width))
-    pad = jnp.zeros((8, 128), F32)
     copies = []
     for side in range(2):
         target = 127 * side
         near = lane < 3 if side == 0 else lane >= 125
-        for m in range(9):
-            tall[side, m, 0:8, :] = pad
-            tall[side, m, height + 8 : height + 16, :] = pad
         for r in range(tiles):
             group, half = r // 2, r % 2
             strip = slice(8 * half, 8 * half + 8)
@@ -489,26 +543,23 @@
                 else:
                     new[side, m, rows, :] = value
                 fix = turned(fixes[side, strip, :], 125 * side - 32 * group - 3 * m, 1)
-                tall[side, m, 8 * r + 8 : 8 * r + 16, :] = swept[m, 8 * r + 8 : 8 * r + 16, columns[side]] + jnp.where(near, fix, 0.0)
+                tall[side, m, rows, :] = swept[m, rows, columns[side]] + jnp.where(near, fix, 0.0)
         copies.append(pltpu.make_async_copy(new.at[side, :, inner], updated.at[:, inner, columns[side]], sems.at[side]))
         copies[-1].start()
 
-    def body(a, carry):
-        for side in range(2):
-            for r in range(tiles):
-
-                def taken(d, k):
-                    return tall[side, 3 * a + d, 8 * r + 8 + k : 8 * r + 16 + k, :]
-
-                for b, value in enumerate(sweep([0, 1, 2], taken)):
-                    if r in (0, tiles - 1):
-                        edges[side, 0 if r == 0 else 1, 9 + 3 * a + b] = value
-                    else:
-                        out[side, 3 * a + b, 8 * r : 8 * r + 8, :] = value
-        return carry
-
-    lax.fori_loop(0, 3, body, 0)
     for side in range(2):
+
+        def body(a, carry, side=side):
+            def store(b, r, value):
+                if r in (0, tiles - 1):
+                    edges[side, 0 if r == 0 else 1, 9 + 3 * a + b] = value
+                else:
+                    out[side, 3 * a + b, 8 * r : 8 * r + 8, :] = value
+
+            sweep_rows(tiles, lambda d, r: tall[side, 3 * a + d, 8 * r : 8 * r + 8, :], store)
+            return carry
+
+        lax.fori_loop(0, 3, body, 0)
         copies.append(pltpu.make_async_copy(out.at[side, :, inner], filtered.at[:, inner, columns[side]], sems.at[2 + side]))
         copies[-1].start()
     for copy in copies:
@@ -583,32 +634,37 @@
     )(*inputs)
     x_odd, x_even = swap_pairs(lax.axis_size("gx"), 1), swap_pairs(lax.axis_size("gx"), 0)
     y_odd, y_even = swap_pairs(lax.axis_size("gy"), 1), swap_pairs(lax.axis_size("gy"), 0)
+    got_even = lax.ppermute(send_even, "gx", x_even)
     got_odd = lax.ppermute(send_odd, "gx", x_odd)
-    got_even = lax.ppermute(send_even, "gx", x_even)
-    updated, filtered, part, swept, traces, middle = call(
-        functools.partial(interior_kernel, width, height),
-        (
-            full,
-            full,
-            shape((2, 9, height, 128), F32),
-            shape((9, height + 16, width), F32),
-            shape((8, width), F32),
-            shape((2, 18, 8, width - 256), F32),
-        ),
-        (120_000_000, 5_000_000),
-        in_specs=[HBM] * 4,
-        out_specs=(HBM, HBM) + (VMEM,) * 4,
-        scratch_shapes=[
-            pltpu.VMEM((9, height, width), F32),
-            pltpu.VMEM((9, height, width), F32),
-            pltpu.VMEM((height, width), F32),
-            pltpu.VMEM((height, width), F32),
-            pltpu.VMEM((3, height + 8, width), F32),
-            pltpu.VMEM((9, height, width - 256), F32),
-            pltpu.VMEM((9, height, width - 256), F32),
-            DMA((14,)),
-        ],
-    )(*inputs)
+    local = (
+        full,
+        full,
+        shape((2, 9, height, 128), F32),
+        full,
+        shape((8, width), F32),
+        shape((2, 18, 8, width - 256), F32),
+    )
+    made = ()
+    for early in (True, False):
+        made = call(
+            functools.partial(interior_kernel, width, height, early),
+            local,
+            (120_000_000, 5_000_000),
+            in_specs=[HBM] * 4 + ([] if early else [HBM] * 2 + [VMEM] * 4),
+            out_specs=(HBM, HBM) + (VMEM,) * 4,
+            input_output_aliases={} if early else {4 + n: n for n in range(6)},
+            scratch_shapes=[
+                pltpu.VMEM((9, height, width), F32),
+                pltpu.VMEM((9, height, width), F32),
+                pltpu.VMEM((height, width), F32),
+                pltpu.VMEM((height, width), F32),
+                pltpu.VMEM((3, height + 8, width), F32),
+                pltpu.VMEM((9, height, width - 256), F32),
+                pltpu.VMEM((9, height, width - 256), F32),
+                DMA((14,)),
+            ],
+        )(*inputs, *made)
+    updated, filtered, part, swept, traces, middle = made
     tall = shape((24, width + 128), F32)
     whole = lambda *dims: pl.BlockSpec(dims, lambda i: (0,) * len(dims))
     send_y_even, send_y_odd, fixes = call(
@@ -618,8 +674,8 @@
         grid=(1,),
         in_specs=[whole(16, 128)] * 4
         + [
-            pl.BlockSpec((9, 8, width), lambda i: (0, 1, 0)),
-            pl.BlockSpec((9, 8, width), lambda i: (0, height // 8, 0)),
+            pl.BlockSpec((9, 8, width), lambda i: (0, 0, 0)),
+            pl.BlockSpec((9, 8, width), lambda i: (0, height // 8 - 1, 0)),
             whole(8, width),
             whole(2, 128, 256),
         ],
@@ -638,7 +694,7 @@
         scratch_shapes=[
             pltpu.VMEM((2, 9, height, 128), F32),
             pltpu.VMEM((2, 9, height, 128), F32),
-            pltpu.VMEM((2, 9, height + 16, 128), F32),
+            pltpu.VMEM((2, 9, height, 128), F32),
             DMA((4,)),
         ],
     )(part, swept, fixes, updated, filtered)

time: 42.4 us -> 41.9 us (0.988)
    pallas_call x1 -> x2, Pallas kernels: 6.66 us -> 6.06 us  [per_device(): call(functools.partial(interior_kernel, width, height, early), local, (12...]
  transfers between devices with their start and end apart: 4 -> 4, of which waited for: 1 -> 1; matrix products, arithmetic and copies ran while one was open for 0% -> 0% of each run, Pallas kernels for 20% -> 19%
where the time goes in v2:
time: 41.9 us; the launch traced here: 41.6 us
  starting transfers between devices  25.2 us (60%)
  Pallas kernels  12.3 us (29%)
  waiting for transfers between devices  3.36 us (8%)
  between operations  0.75 us (2%)
    ppermute x1, starting transfers between devices, per_device(): got_even = lax.ppermute(send_even, 'gx', x_even)  11.4 us
    ppermute x1, starting transfers between devices, per_device(): got_odd = lax.ppermute(send_odd, 'gx', x_odd)  6.24 us
    pallas_call x2, Pallas kernels, per_device(): call(functools.partial(interior_kernel, width, height, early), local, (12...  6.06 us
    ppermute x1, starting transfers between devices, per_device(): got_y_odd = lax.ppermute(send_y_odd, 'gy', y_odd)  4.36 us
    ppermute x1, waiting for transfers between devices, per_device(): got_y_odd = lax.ppermute(send_y_odd, 'gy', y_odd)  3.35 us
    ppermute x1, starting transfers between devices, per_device(): got_y_even = lax.ppermute(send_y_even, 'gy', y_even)  3.14 us
    pallas_call x1, Pallas kernels, per_device(): call(functools.partial(pack_kernel, width, height), (pack,) * 4, (2000000...  2.71 us
    pallas_call x1, Pallas kernels, per_device(): call(functools.partial(finish_kernel, width, height), (full, full, shape(...  1.7 us
  transfers between devices with their start and end apart: 4, of which 1 were waited for; matrix products, arithmetic and copies ran while one was open for 0% of the time, Pallas kernels for 19%

profile of v2, /device:TPU:63, one launch (start us, length us, event | category | flops | bytes accessed | tf_op | source)
XLA Modules:
  0.0 41.6 jit_solution(17184576217769006196)
XLA Ops:
  0.6 2.7 %shard_map.77 = (f32[16,128]{1,0:T(8,128)S(1)}, f32[16,128]{1,0:T(8,128)S(1)}, f32[16,128]{1,0:T(8,128)S(1)}, f32[16,128]{1,0:T(8,128)S(1)}) custom-call(f32[9,64,512]{2,1,0:T(8,128)} %refs_0_.3, f32[9,64,512]{2,1,0:T(8,128)} %refs_1_.3, f32[64,512]{1,0:T(8,128)} %refs_2_.3, f32[64,512]{1,0:T(8,128)} %refs_3_.3), custom_call_target="tpu_custom_call" | custom-call | flops 20000000 | bytes 1400000 | tf_op jit(solution)/shard_map/pallas_call | solution.py:627
  3.3 6.2 %collective-permute-start = (f32[16,128]{1,0:T(8,128)S(1)}, f32[16,128]{1,0:T(8,128)S(1)}, u32[]{:S(2)}, u32[]{:S(2)}) collective-permute-start(f32[16,128]{1,0:T(8,128)S(1)} %get-tuple-element.24), channel_id=1, source_target_pairs={{32,64},{64,32},{96,128},{128,96},{160,192},{192,160},{224,256},{2... | collective-permute-start | bytes 24584 | tf_op jit(solution)/shard_map/ppermute | solution.py:638
  9.6 11.4 %collective-permute-start.1 = (f32[16,128]{1,0:T(8,128)S(1)}, f32[16,128]{1,0:T(8,128)S(1)}, u32[]{:S(2)}, u32[]{:S(2)}) collective-permute-start(f32[16,128]{1,0:T(8,128)S(1)} %get-tuple-element.25), channel_id=1, source_target_pairs={{0,32},{32,0},{64,96},{96,64},{128,160},{160,128},{192,224},{224,1... | collective-permute-start | bytes 24584 | tf_op jit(solution)/shard_map/ppermute | solution.py:637
  21.0 0.1 shard_map.78
  21.2 0.0 copy-start
  21.2 5.9 %shard_map.79 = (f32[9,64,512]{2,1,0:T(8,128)}, f32[9,64,512]{2,1,0:T(8,128)}, f32[2,9,64,128]{3,2,1,0:T(8,128)S(1)}, f32[9,64,512]{2,1,0:T(8,128)S(1)}, f32[8,5...) custom-call(f32[9,64,512]{2,1,0:T(8,128)} %refs_0_.3, ...), custom_call_target="tpu_custom_call", output_to_operand_aliasing={{0}: (4, {}), {1}: (5, {}), {2}: (6, {}), {3}: (7, {}), {4}... | custom-call | flops 120000000 | bytes 5000000 | tf_op jit(solution)/shard_map/pallas_call | solution.py:649
  27.1 0.0 collective-permute-done.got_odd
  27.1 0.0 collective-permute-done.1.got_even
  27.1 0.0 copy-done
  27.1 0.4 shard_map.80
  27.6 3.1 %collective-permute-start.2 = (f32[24,640]{1,0:T(8,128)S(1)}, f32[24,640]{1,0:T(8,128)S(1)}, u32[]{:S(2)}, u32[]{:S(2)}) collective-permute-start(f32[24,640]{1,0:T(8,128)S(1)} %get-tuple-element.36.sent_even), channel_id=1, source_target_pairs={{0,1},{1,0},{2,3},{3,2},{4,5},{5,4},{6,7},{7,6},{8,9},{9,8},{10,11... | collective-permute-start | bytes 184328 | tf_op jit(solution)/shard_map/ppermute | solution.py:685
  30.7 4.4 %collective-permute-start.3 = (f32[24,640]{1,0:T(8,128)S(1)}, f32[24,640]{1,0:T(8,128)S(1)}, u32[]{:S(2)}, u32[]{:S(2)}) collective-permute-start(f32[24,640]{1,0:T(8,128)S(1)} %get-tuple-element.37.sent_odd), channel_id=1, source_target_pairs={{1,2},{2,1},{3,4},{4,3},{5,6},{6,5},{7,8},{8,7},{9,10},{10,9},{11,... | collective-permute-start | bytes 184328 | tf_op jit(solution)/shard_map/ppermute | solution.py:686
  35.1 0.0 copy-start.1
  35.1 1.7 %shard_map.81 = (f32[9,64,512]{2,1,0:T(8,128)}, f32[9,64,512]{2,1,0:T(8,128)}, f32[2,2,18,8,128]{4,3,2,1,0:T(8,128)S(1)}) custom-call(f32[2,9,64,128]{3,2,1,0:T(8,128)S(1)} %get-tuple-element.39.part, f32[9,64,512]{2,1,0:T(8,128)S(1)} %get-tuple-element.34.low_rows.high_rows.swept, ...), custom_call_target="tpu_custom_call", output_to_operand_aliasing={{0}: (3, {}), {1}: (4, {})} | custom-call | flops 60000000 | bytes 4000000 | tf_op jit(solution)/shard_map/pallas_call | solution.py:687
  36.8 0.0 collective-permute-done.2.got_even
  36.8 3.3 %collective-permute-done.3.got_odd = f32[24,640]{1,0:T(8,128)S(1)} collective-permute-done((f32[24,640]{1,0:T(8,128)S(1)}, f32[24,640]{1,0:T(8,128)S(1)}, u32[]{:S(2)}, u32[]{:S(2)}) %collective-permute-start.3) | collective-permute-done | bytes 61472 | tf_op jit(solution)/shard_map/ppermute | solution.py:686
  40.2 0.0 copy-done.1
  40.2 1.4 %shard_map.82 = (f32[9,64,512]{2,1,0:T(8,128)}, f32[9,64,512]{2,1,0:T(8,128)}) custom-call(f32[24,640]{1,0:T(8,128)S(1)} %collective-permute-done.2.got_even, f32[24,640]{1,0:T(8,128)S(1)} %collective-permute-done.3.got_odd, f32[24,640]{1,0:T(8,128)S(1)} %get-tuple-element.36.sent_even, ...), custom_call_target="tpu_custom_call", output_to_operand_aliasing={{0}: (7, {}), {1}: (8, {})} | custom-call | flops 4000000 | bytes 1000000 | tf_op jit(solution)/shard_map/pallas_call | solution.py:701
Async XLA Ops:
  3.3 23.8 %collective-permute-start = (f32[16,128]{1,0:T(8,128)S(1)}, f32[16,128]{1,0:T(8,128)S(1)}, u32[]{:S(2)}, u32[]{:S(2)}) collective-permute-start(f32[16,128]{1,0:T(8,128)S(1)} %get-tuple-element.24), channel_id=1, source_target_pairs={{32,64},{64,32},{96,128},{128,96},{160,192},{192,160},{224,256},{2... | collective-permute-start | bytes 24584 | tf_op jit(solution)/shard_map/ppermute | solution.py:638
  9.6 17.5 %collective-permute-start.1 = (f32[16,128]{1,0:T(8,128)S(1)}, f32[16,128]{1,0:T(8,128)S(1)}, u32[]{:S(2)}, u32[]{:S(2)}) collective-permute-start(f32[16,128]{1,0:T(8,128)S(1)} %get-tuple-element.25), channel_id=1, source_target_pairs={{0,32},{32,0},{64,96},{96,64},{128,160},{160,128},{192,224},{224,1... | collective-permute-start | bytes 24584 | tf_op jit(solution)/shard_map/ppermute | solution.py:637
  21.2 6.0 %copy-start = (f32[2,128,256]{2,1,0:T(8,128)S(1)}, f32[2,128,256]{2,1,0:T(8,128)}, u32[]{:S(2)}) copy-start(f32[2,128,256]{2,1,0:T(8,128)} %constant.4.clone.matrices) | copy-start | bytes 786436
  27.6 9.2 %collective-permute-start.2 = (f32[24,640]{1,0:T(8,128)S(1)}, f32[24,640]{1,0:T(8,128)S(1)}, u32[]{:S(2)}, u32[]{:S(2)}) collective-permute-start(f32[24,640]{1,0:T(8,128)S(1)} %get-tuple-element.36.sent_even), channel_id=1, source_target_pairs={{0,1},{1,0},{2,3},{3,2},{4,5},{5,4},{6,7},{7,6},{8,9},{9,8},{10,11... | collective-permute-start | bytes 184328 | tf_op jit(solution)/shard_map/ppermute | solution.py:685
  30.7 9.4 %collective-permute-start.3 = (f32[24,640]{1,0:T(8,128)S(1)}, f32[24,640]{1,0:T(8,128)S(1)}, u32[]{:S(2)}, u32[]{:S(2)}) collective-permute-start(f32[24,640]{1,0:T(8,128)S(1)} %get-tuple-element.37.sent_odd), channel_id=1, source_target_pairs={{1,2},{2,1},{3,4},{4,3},{5,6},{6,5},{7,8},{8,7},{9,10},{10,9},{11,... | collective-permute-start | bytes 184328 | tf_op jit(solution)/shard_map/ppermute | solution.py:686
  35.1 5.1 %copy-start.1 = (f32[2,144,64]{2,1,0:T(8,128)S(1)}, f32[2,144,64]{2,1,0:T(8,128)}, u32[]{:S(2)}) copy-start(f32[2,144,64]{2,1,0:T(8,128)} %constant.5.clone.matrices) | copy-start | bytes 221188

commit v3 on v2

--- a/solution.py
+++ b/solution.py
@@ -279,21 +279,32 @@
             store(b, r, value)
 
 
-def interior_kernel(width, height, early, *refs):
-    inputs, rest = refs[:4], refs[4 if early else 10 :]
-
-    @pl.when((lax.axis_index("gx") == 0) == early)
+def early_kernel(width, height, start, sect, vel_x, vel_y, new, part, swept, traces, s, u, vx, vy, south, sems):
+    @pl.when(lax.axis_index("gx") == 0)
     def _():
-        interior(width, height, *inputs, *rest)
-
-
-def interior(
-    width, height, start, sect, vel_x, vel_y, updated, filtered, part, swept, traces, edges, s, u, vx, vy, south, new, out, sems
-):
+        local_part(width, height, start, sect, vel_x, vel_y, new, part, swept, traces, s, u, vx, vy, south, sems)
+
+
+def late_kernel(width, height, *refs):
+    inputs, made, (part, swept, traces), outs = refs[:4], refs[4:8], refs[8:11], refs[11:14]
+    s, u, vx, vy, south, new, out, sems = refs[14:]
+    column = lax.axis_index("gx")
+
+    @pl.when(column != 0)
+    def _():
+        local_part(width, height, *inputs, new, part, swept, traces, s, u, vx, vy, south, sems)
+
+    @pl.when(column == 0)
+    def _():
+        for source, target in zip(made, (new, part, swept, traces)):
+            target[...] = source[...]
+
+    middle_part(width, height, new, swept, *outs, out, sems)
+
+
+def local_part(width, height, start, sect, vel_x, vel_y, new, part, swept, traces, s, u, vx, vy, south, sems):
     middle = slice(128, width - 128)
-    inner = slice(8, height - 8)
     chunk = 16
-    tiles = height // 8
     shape = (8, width)
     lane = tile_iota(shape, 1)
     sub = tile_iota(shape, 0)
@@ -411,6 +422,12 @@
     for n in range(height // chunk):
         begin[n].wait()
         lax.fori_loop(n * chunk // 8, (n + 1) * chunk // 8, cells, 0)
+
+
+def middle_part(width, height, new, swept, updated, filtered, edges, out, sems):
+    middle = slice(128, width - 128)
+    inner = slice(8, height - 8)
+    tiles = height // 8
     new_copy = pltpu.make_async_copy(new.at[:, inner], updated.at[:, inner, middle], sems.at[10])
     new_copy.start()
     for m in range(9):
@@ -435,7 +452,7 @@
             sweep_rows(tiles, lambda d, r: swept[3 * a + d, 8 * r : 8 * r + 8, source], store)
             return carry
 
-        lax.fori_loop(0, pieces - 2, column, 0)
+        lax.fori_loop(0, width // 128 - 2, column, 0)
         out_copy(a).start()
         return carry
 
@@ -636,35 +653,36 @@
     y_odd, y_even = swap_pairs(lax.axis_size("gy"), 1), swap_pairs(lax.axis_size("gy"), 0)
     got_even = lax.ppermute(send_even, "gx", x_even)
     got_odd = lax.ppermute(send_odd, "gx", x_odd)
-    local = (
-        full,
-        full,
-        shape((2, 9, height, 128), F32),
-        full,
-        shape((8, width), F32),
-        shape((2, 18, 8, width - 256), F32),
-    )
-    made = ()
-    for early in (True, False):
-        made = call(
-            functools.partial(interior_kernel, width, height, early),
-            local,
-            (120_000_000, 5_000_000),
-            in_specs=[HBM] * 4 + ([] if early else [HBM] * 2 + [VMEM] * 4),
-            out_specs=(HBM, HBM) + (VMEM,) * 4,
-            input_output_aliases={} if early else {4 + n: n for n in range(6)},
-            scratch_shapes=[
-                pltpu.VMEM((9, height, width), F32),
-                pltpu.VMEM((9, height, width), F32),
-                pltpu.VMEM((height, width), F32),
-                pltpu.VMEM((height, width), F32),
-                pltpu.VMEM((3, height + 8, width), F32),
-                pltpu.VMEM((9, height, width - 256), F32),
-                pltpu.VMEM((9, height, width - 256), F32),
-                DMA((14,)),
-            ],
-        )(*inputs, *made)
-    updated, filtered, part, swept, traces, middle = made
+    local = (shape((2, 9, height, 128), F32), full, shape((8, width), F32))
+    inner = shape((9, height, width - 256), F32)
+    room = [
+        pltpu.VMEM((9, height, width), F32),
+        pltpu.VMEM((9, height, width), F32),
+        pltpu.VMEM((height, width), F32),
+        pltpu.VMEM((height, width), F32),
+        pltpu.VMEM((3, height + 8, width), F32),
+    ]
+    made = call(
+        functools.partial(early_kernel, width, height),
+        (inner, *local),
+        (100_000_000, 5_000_000),
+        in_specs=[HBM] * 4,
+        out_specs=(VMEM,) * 4,
+        scratch_shapes=[*room, DMA((14,))],
+    )(*inputs)
+    part, swept, traces, updated, filtered, middle = call(
+        functools.partial(late_kernel, width, height),
+        (*local, full, full, shape((2, 18, 8, width - 256), F32)),
+        (120_000_000, 5_000_000),
+        in_specs=[HBM] * 4 + [VMEM] * 4,
+        out_specs=(VMEM, VMEM, VMEM, HBM, HBM, VMEM),
+        scratch_shapes=[
+            *room,
+            pltpu.VMEM((9, height, width - 256), F32),
+            pltpu.VMEM((9, height, width - 256), F32),
+            DMA((14,)),
+        ],
+    )(*inputs, *made)
     tall = shape((24, width + 128), F32)
     whole = lambda *dims: pl.BlockSpec(dims, lambda i: (0,) * len(dims))
     send_y_even, send_y_odd, fixes = call(

time: 41.9 us -> 41.9 us (level)
  no operation moved by 1% of the time
where the time goes in v3:
time: 41.9 us; the launch traced here: 41.6 us
  starting transfers between devices  25.2 us (60%)
  Pallas kernels  12.3 us (29%)
  waiting for transfers between devices  3.36 us (8%)
  between operations  0.75 us (2%)
    ppermute x1, starting transfers between devices, per_device(): got_even = lax.ppermute(send_even, 'gx', x_even)  11.4 us
    ppermute x1, starting transfers between devices, per_device(): got_odd = lax.ppermute(send_odd, 'gx', x_odd)  6.24 us
    pallas_call x1, Pallas kernels, per_device(): call(functools.partial(late_kernel, width, height), (*local, full, full,...  5.93 us
    ppermute x1, starting transfers between devices, per_device(): got_y_odd = lax.ppermute(send_y_odd, 'gy', y_odd)  4.36 us
    ppermute x1, waiting for transfers between devices, per_device(): got_y_odd = lax.ppermute(send_y_odd, 'gy', y_odd)  3.35 us
    ppermute x1, starting transfers between devices, per_device(): got_y_even = lax.ppermute(send_y_even, 'gy', y_even)  3.14 us
    pallas_call x1, Pallas kernels, per_device(): call(functools.partial(pack_kernel, width, height), (pack,) * 4, (2000000...  2.71 us
    pallas_call x1, Pallas kernels, per_device(): call(functools.partial(finish_kernel, width, height), (full, full, shape(...  1.7 us
  transfers between devices with their start and end apart: 4, of which 1 were waited for; matrix products, arithmetic and copies ran while one was open for 0% of the time, Pallas kernels for 19%

profile of v3, /device:TPU:63, one launch (start us, length us, event | category | flops | bytes accessed | tf_op | source)
XLA Modules:
  0.0 41.6 jit_solution(11568573260994591851)
XLA Ops:
  0.6 2.7 %shard_map.77 = (f32[16,128]{1,0:T(8,128)S(1)}, f32[16,128]{1,0:T(8,128)S(1)}, f32[16,128]{1,0:T(8,128)S(1)}, f32[16,128]{1,0:T(8,128)S(1)}) custom-call(f32[9,64,512]{2,1,0:T(8,128)} %refs_0_.1, f32[9,64,512]{2,1,0:T(8,128)} %refs_1_.1, f32[64,512]{1,0:T(8,128)} %refs_2_.1, f32[64,512]{1,0:T(8,128)} %refs_3_.1), custom_call_target="tpu_custom_call" | custom-call | flops 20000000 | bytes 1400000 | tf_op jit(solution)/shard_map/pallas_call | solution.py:644
  3.3 6.2 %collective-permute-start = (f32[16,128]{1,0:T(8,128)S(1)}, f32[16,128]{1,0:T(8,128)S(1)}, u32[]{:S(2)}, u32[]{:S(2)}) collective-permute-start(f32[16,128]{1,0:T(8,128)S(1)} %get-tuple-element.22), channel_id=1, source_target_pairs={{32,64},{64,32},{96,128},{128,96},{160,192},{192,160},{224,256},{2... | collective-permute-start | bytes 24584 | tf_op jit(solution)/shard_map/ppermute | solution.py:655
  9.6 11.4 %collective-permute-start.1 = (f32[16,128]{1,0:T(8,128)S(1)}, f32[16,128]{1,0:T(8,128)S(1)}, u32[]{:S(2)}, u32[]{:S(2)}) collective-permute-start(f32[16,128]{1,0:T(8,128)S(1)} %get-tuple-element.23), channel_id=1, source_target_pairs={{0,32},{32,0},{64,96},{96,64},{128,160},{160,128},{192,224},{224,1... | collective-permute-start | bytes 24584 | tf_op jit(solution)/shard_map/ppermute | solution.py:654
  21.0 0.1 shard_map.78
  21.2 0.0 copy-start
  21.2 5.9 %shard_map.79 = (f32[2,9,64,128]{3,2,1,0:T(8,128)S(1)}, f32[9,64,512]{2,1,0:T(8,128)S(1)}, f32[8,512]{1,0:T(8,128)S(1)}, f32[9,64,512]{2,1,0:T(8,128)}, f32[9,64...) custom-call(f32[9,64,512]{2,1,0:T(8,128)} %refs_0_.1, f32[9,64,512]{2,1,0:T(8,128)} %refs_1_.1, f32[64,512]{1,0:T(8,128)} %refs_2_.1, ...), custom_call_target="tpu_custom_call" | custom-call | flops 120000000 | bytes 5000000 | tf_op jit(solution)/shard_map/pallas_call | solution.py:673
  27.1 0.0 collective-permute-done.got_odd
  27.1 0.0 collective-permute-done.1.got_even
  27.1 0.0 copy-done
  27.2 0.4 shard_map.80
  27.6 3.1 %collective-permute-start.2 = (f32[24,640]{1,0:T(8,128)S(1)}, f32[24,640]{1,0:T(8,128)S(1)}, u32[]{:S(2)}, u32[]{:S(2)}) collective-permute-start(f32[24,640]{1,0:T(8,128)S(1)} %get-tuple-element.32.sent_even), channel_id=1, source_target_pairs={{0,1},{1,0},{2,3},{3,2},{4,5},{5,4},{6,7},{7,6},{8,9},{9,8},{10,11... | collective-permute-start | bytes 184328 | tf_op jit(solution)/shard_map/ppermute | solution.py:703
  30.7 4.4 %collective-permute-start.3 = (f32[24,640]{1,0:T(8,128)S(1)}, f32[24,640]{1,0:T(8,128)S(1)}, u32[]{:S(2)}, u32[]{:S(2)}) collective-permute-start(f32[24,640]{1,0:T(8,128)S(1)} %get-tuple-element.33.sent_odd), channel_id=1, source_target_pairs={{1,2},{2,1},{3,4},{4,3},{5,6},{6,5},{7,8},{8,7},{9,10},{10,9},{11,... | collective-permute-start | bytes 184328 | tf_op jit(solution)/shard_map/ppermute | solution.py:704
  35.1 0.0 copy-start.1
  35.1 1.7 %shard_map.81 = (f32[9,64,512]{2,1,0:T(8,128)}, f32[9,64,512]{2,1,0:T(8,128)}, f32[2,2,18,8,128]{4,3,2,1,0:T(8,128)S(1)}) custom-call(f32[2,9,64,128]{3,2,1,0:T(8,128)S(1)} %get-tuple-element.35.part, f32[9,64,512]{2,1,0:T(8,128)S(1)} %get-tuple-element.30.low_rows.high_rows.swept, ...), custom_call_target="tpu_custom_call", output_to_operand_aliasing={{0}: (3, {}), {1}: (4, {})} | custom-call | flops 60000000 | bytes 4000000 | tf_op jit(solution)/shard_map/pallas_call | solution.py:705
  36.8 0.0 collective-permute-done.2.got_even
  36.8 3.3 %collective-permute-done.3.got_odd = f32[24,640]{1,0:T(8,128)S(1)} collective-permute-done((f32[24,640]{1,0:T(8,128)S(1)}, f32[24,640]{1,0:T(8,128)S(1)}, u32[]{:S(2)}, u32[]{:S(2)}) %collective-permute-start.3) | collective-permute-done | bytes 61472 | tf_op jit(solution)/shard_map/ppermute | solution.py:704
  40.2 0.0 copy-done.1
  40.2 1.4 %shard_map.82 = (f32[9,64,512]{2,1,0:T(8,128)}, f32[9,64,512]{2,1,0:T(8,128)}) custom-call(f32[24,640]{1,0:T(8,128)S(1)} %collective-permute-done.2.got_even, f32[24,640]{1,0:T(8,128)S(1)} %collective-permute-done.3.got_odd, f32[24,640]{1,0:T(8,128)S(1)} %get-tuple-element.32.sent_even, ...), custom_call_target="tpu_custom_call", output_to_operand_aliasing={{0}: (7, {}), {1}: (8, {})} | custom-call | flops 4000000 | bytes 1000000 | tf_op jit(solution)/shard_map/pallas_call | solution.py:719
Async XLA Ops:
  3.3 23.8 %collective-permute-start = (f32[16,128]{1,0:T(8,128)S(1)}, f32[16,128]{1,0:T(8,128)S(1)}, u32[]{:S(2)}, u32[]{:S(2)}) collective-permute-start(f32[16,128]{1,0:T(8,128)S(1)} %get-tuple-element.22), channel_id=1, source_target_pairs={{32,64},{64,32},{96,128},{128,96},{160,192},{192,160},{224,256},{2... | collective-permute-start | bytes 24584 | tf_op jit(solution)/shard_map/ppermute | solution.py:655
  9.6 17.5 %collective-permute-start.1 = (f32[16,128]{1,0:T(8,128)S(1)}, f32[16,128]{1,0:T(8,128)S(1)}, u32[]{:S(2)}, u32[]{:S(2)}) collective-permute-start(f32[16,128]{1,0:T(8,128)S(1)} %get-tuple-element.23), channel_id=1, source_target_pairs={{0,32},{32,0},{64,96},{96,64},{128,160},{160,128},{192,224},{224,1... | collective-permute-start | bytes 24584 | tf_op jit(solution)/shard_map/ppermute | solution.py:654
  21.2 6.0 %copy-start = (f32[2,128,256]{2,1,0:T(8,128)S(1)}, f32[2,128,256]{2,1,0:T(8,128)}, u32[]{:S(2)}) copy-start(f32[2,128,256]{2,1,0:T(8,128)} %constant.4.clone.matrices) | copy-start | bytes 786436
  27.6 9.2 %collective-permute-start.2 = (f32[24,640]{1,0:T(8,128)S(1)}, f32[24,640]{1,0:T(8,128)S(1)}, u32[]{:S(2)}, u32[]{:S(2)}) collective-permute-start(f32[24,640]{1,0:T(8,128)S(1)} %get-tuple-element.32.sent_even), channel_id=1, source_target_pairs={{0,1},{1,0},{2,3},{3,2},{4,5},{5,4},{6,7},{7,6},{8,9},{9,8},{10,11... | collective-permute-start | bytes 184328 | tf_op jit(solution)/shard_map/ppermute | solution.py:703
  30.7 9.4 %collective-permute-start.3 = (f32[24,640]{1,0:T(8,128)S(1)}, f32[24,640]{1,0:T(8,128)S(1)}, u32[]{:S(2)}, u32[]{:S(2)}) collective-permute-start(f32[24,640]{1,0:T(8,128)S(1)} %get-tuple-element.33.sent_odd), channel_id=1, source_target_pairs={{1,2},{2,1},{3,4},{4,3},{5,6},{6,5},{7,8},{8,7},{9,10},{10,9},{11,... | collective-permute-start | bytes 184328 | tf_op jit(solution)/shard_map/ppermute | solution.py:704
  35.1 5.1 %copy-start.1 = (f32[2,144,64]{2,1,0:T(8,128)S(1)}, f32[2,144,64]{2,1,0:T(8,128)}, u32[]{:S(2)}) copy-start(f32[2,144,64]{2,1,0:T(8,128)} %constant.5.clone.matrices) | copy-start | bytes 221188
